TPU v7x, 32 devices: a whole 2x2x4 slice. The times are simulated.
32 devices in a mesh: row: 8 (over y, x, core), col: 4 (over z).
Axes of the slice: x: 2, y: 2, z: 4, core: 2. Of those that a mesh axis runs over, the one named last changes fastest.
Arguments:
- block_input: bfloat16 [8192, 768], P(('row', 'col'))
- block_cotangent: bfloat16 [8192, 768], P(('row', 'col')), may hold values from -6 to 6
- block_lengths: int32 [64], P(('row', 'col')), may hold values from 1 to 128, as said below
- block_offsets: int32 [64], P(('row', 'col')), may hold values from 0 to 128, as said below
- norm1_gain: float32 [768], replicated, may hold values from 0.25 to 1.75
- norm1_bias: float32 [768], replicated, may hold values from -2.5 to 2.5
- norm2_gain: float32 [768], replicated, may hold values from 0.25 to 1.75
- norm2_bias: float32 [768], replicated, may hold values from -2.5 to 2.5
- qkv_weight: bfloat16 [768, 2304], P('row', 'col'), may hold values from -0.21875 to 0.21875
- qkv_bias: float32 [2304], P('col'), may hold values from -3 to 3
- dense_weight: bfloat16 [768, 768], P('col', 'row'), may hold values from -0.875 to 0.875
- dense_bias: float32 [768], replicated, may hold values from -2.5 to 2.5
- fc_in_weight: bfloat16 [768, 3072], P('row', 'col'), may hold values from -0.21875 to 0.21875
- fc_in_bias: float32 [3072], P('col'), may hold values from -3 to 3
- fc_out_weight: bfloat16 [3072, 768], P('col', 'row'), may hold values from -0.109375 to 0.109375
- fc_out_bias: float32 [768], replicated, may hold values from -2.5 to 2.5
Outputs:
- block_out: float32 [8192, 768], P(('row', 'col'))
- input_grad: float32 [8192, 768], P(('row', 'col'))
- norm1_gain_grad: float32 [768], replicated
- norm1_bias_grad: float32 [768], replicated
- norm2_gain_grad: float32 [768], replicated
- norm2_bias_grad: float32 [768], replicated
- qkv_weight_grad: float32 [768, 2304], P('row', 'col')
- qkv_bias_grad: float32 [2304], P('col')
- dense_weight_grad: float32 [768, 768], P('col', 'row')
- dense_bias_grad: float32 [768], replicated
- fc_in_weight_grad: float32 [768, 3072], P('row', 'col')
- fc_in_bias_grad: float32 [3072], P('col')
- fc_out_weight_grad: float32 [3072, 768], P('col', 'row')
- fc_out_bias_grad: float32 [768], replicated
Inputs may be any that keep to these rules, and one draw needn't show every extreme that they name: `block_lengths`: blocks come in aligned pairs. A pair holds either two sequences, each in its own block, or one sequence over both blocks, whose first block is then full. `block_offsets`: an even block's offset is 0; an odd block's is 0 when it starts a sequence and 128 when it continues the sequence of the block before it.
All inputs are finite; a program needn't handle non-finite values.
Results may differ from a plain program's by a relative error of at most 0.0088.
Values may be sent and summed in bfloat16 or wider, within the bound.
A program may use at most 128 MiB of HBM per device.

v0:
```python
import math

import jax
import jax.numpy as jnp
from jax import lax
from jax.sharding import PartitionSpec as P

HEADS = 12
ROT = 16


NORM_EPSILON = 1e-05
HALF_ROOT = math.sqrt(0.5)
DENSITY_SCALE = 1.0 / math.sqrt(2.0 * math.pi)


def normalize(features):
    widened = features.astype(jnp.float32)
    centered = widened - jnp.mean(widened, axis=1, keepdims=True)
    inverse = lax.rsqrt(jnp.mean(centered * centered, axis=1, keepdims=True) + NORM_EPSILON)
    return (centered * inverse, inverse)


def norm_back(grad_normed, gain, standard, inverse):
    grad_unit = grad_normed * gain
    return inverse * (
        grad_unit
        - jnp.mean(grad_unit, axis=1, keepdims=True)
        - standard * jnp.mean(grad_unit * standard, axis=1, keepdims=True)
    )


def gelu_exact(pre_act):
    return 0.5 * pre_act * (1.0 + lax.erf(pre_act * HALF_ROOT))


def gelu_slope(pre_act):
    return (
        0.5 * (1.0 + lax.erf(pre_act * HALF_ROOT))
        + pre_act * jnp.exp(-0.5 * pre_act * pre_act) * DENSITY_SCALE
    )


def rotary_tables(positions, rotated):
    halves = rotated // 2
    frequency = 10000.0 ** (-2.0 * jnp.arange(halves, dtype=jnp.float32) / rotated)
    angles = positions[:, None].astype(jnp.float32) * frequency[None, :]
    angles = jnp.concatenate([angles, angles], axis=1)
    return (jnp.cos(angles)[:, None, :], jnp.sin(angles)[:, None, :])


def rotate(values, cosine, sine_table, rotated):
    halves = rotated // 2
    leading = values[..., :rotated]
    turned = jnp.concatenate([-leading[..., halves:], leading[..., :halves]], axis=-1)
    return jnp.concatenate([leading * cosine + turned * sine_table, values[..., rotated:]], axis=-1)


def unrotate(gradient, cosine, sine_table, rotated):
    halves = rotated // 2
    leading = gradient[..., :rotated]
    scaled = leading * sine_table
    turned = jnp.concatenate([scaled[..., halves:], -scaled[..., :halves]], axis=-1)
    return jnp.concatenate([leading * cosine + turned, gradient[..., rotated:]], axis=-1)


def pair_mask(lengths, offsets, block_rows):
    pair_count = lengths.shape[0] // 2
    local_rows = jnp.arange(2 * block_rows, dtype=jnp.int32)
    block_of = local_rows // block_rows
    in_block = local_rows % block_rows
    pair_lengths = lengths.reshape(pair_count, 2)
    joined = offsets.reshape(pair_count, 2)[:, 1] > 0
    row_limit = jnp.where(block_of[None, :] == 0, pair_lengths[:, 0:1], pair_lengths[:, 1:2])
    live_keys = in_block[None, :] < row_limit
    same_seq = (block_of[:, None] == block_of[None, :])[None, :, :] | joined[:, None, None]
    causal = (local_rows[None, :] <= local_rows[:, None])[None, :, :]
    diagonal = (local_rows[:, None] == local_rows[None, :])[None, :, :]
    return same_seq & causal & (live_keys[:, None, :] | diagonal)


def masked_scores(queries, key_rows, allowed, score_scale):
    scores = (
        jnp.einsum("pihd,pjhd->phij", queries, key_rows, preferred_element_type=jnp.float32)
        * score_scale
    )
    return jnp.where(allowed[:, None, :, :], scores, -jnp.inf)


def on_device(
    block_input,
    block_cotangent,
    block_lengths,
    block_offsets,
    norm1_gain,
    norm1_bias,
    norm2_gain,
    norm2_bias,
    qkv_weight,
    qkv_bias,
    dense_weight,
    dense_bias,
    fc_in_weight,
    fc_in_bias,
    fc_out_weight,
    fc_out_bias,
):
    groups = lax.axis_size("col")
    col_index = lax.axis_index("col")
    own_rows = block_input.shape[0]
    width = block_input.shape[1]
    head_dim = width // HEADS
    block_count = block_lengths.shape[0]
    block_rows = own_rows // block_count
    pair_count = block_count // 2
    four_shape = (pair_count, 2 * block_rows, HEADS, head_dim)
    score_scale = head_dim ** (-0.5)
    contract_rows = (((0,), (0,)), ((), ()))
    in_block = jnp.arange(block_rows, dtype=jnp.int32)
    positions = (block_offsets[:, None] + in_block[None, :]).reshape(-1)
    valid = (in_block[None, :] < block_lengths[:, None]).reshape(-1)
    cosine, sine_table = rotary_tables(positions, ROT)
    allowed = pair_mask(block_lengths, block_offsets, block_rows)
    standard, inverse = normalize(block_input)
    normed_first = (standard * norm1_gain + norm1_bias).astype(jnp.bfloat16)
    normed_second = (standard * norm2_gain + norm2_bias).astype(jnp.bfloat16)
    first_rows, second_rows = (
        lax.all_gather(normed_first, "col", axis=0, tiled=True),
        lax.all_gather(normed_second, "col", axis=0, tiled=True),
    )
    qkv_block, fc_in_block, dense_block, fc_out_block = (
        lax.all_gather(qkv_weight, "row", axis=0, tiled=True),
        lax.all_gather(fc_in_weight, "row", axis=0, tiled=True),
        lax.all_gather(dense_weight, "row", axis=1, tiled=True),
        lax.all_gather(fc_out_weight, "row", axis=1, tiled=True),
    )
    mixed_rows = (
        jnp.dot(first_rows, qkv_block, preferred_element_type=jnp.float32) + qkv_bias
    ).astype(jnp.bfloat16)
    mixed_own = lax.all_to_all(mixed_rows, "col", split_axis=0, concat_axis=1, tiled=True)
    mixed_own = mixed_own.reshape(own_rows, 3, HEADS, head_dim)
    queries = rotate(mixed_own[:, 0].astype(jnp.float32), cosine, sine_table, ROT).astype(
        jnp.bfloat16
    )
    key_rows = rotate(mixed_own[:, 1].astype(jnp.float32), cosine, sine_table, ROT).astype(
        jnp.bfloat16
    )
    queries = queries.reshape(four_shape)
    key_rows = key_rows.reshape(four_shape)
    values = mixed_own[:, 2].reshape(four_shape)
    scores = masked_scores(queries, key_rows, allowed, score_scale)
    highest = jnp.max(scores, axis=-1, keepdims=True)
    totals = highest + jnp.log(jnp.sum(jnp.exp(scores - highest), axis=-1, keepdims=True))
    weights = jnp.exp(scores - totals).astype(jnp.bfloat16)
    attended = jnp.einsum("phij,pjhd->pihd", weights, values, preferred_element_type=jnp.float32)
    attended = attended.astype(jnp.bfloat16).reshape(own_rows, width)
    attended_rows = lax.all_to_all(attended, "col", split_axis=1, concat_axis=0, tiled=True)
    pre_act = jnp.dot(second_rows, fc_in_block, preferred_element_type=jnp.float32) + fc_in_bias
    hidden = gelu_exact(pre_act).astype(jnp.bfloat16)
    summed = lax.psum_scatter(
        (
            jnp.dot(attended_rows, dense_block, preferred_element_type=jnp.float32)
            + jnp.dot(hidden, fc_out_block, preferred_element_type=jnp.float32)
        ).astype(jnp.bfloat16),
        "col",
        scatter_dimension=0,
        tiled=True,
    ).astype(jnp.float32)
    block_out = block_input.astype(jnp.float32) + dense_bias + fc_out_bias + summed
    grad_out = jnp.where(valid[:, None], block_cotangent, jnp.zeros_like(block_cotangent))
    grad_rows = lax.all_gather(grad_out, "col", axis=0, tiled=True)
    grad_hidden = jnp.dot(grad_rows, fc_out_block.T, preferred_element_type=jnp.float32)
    grad_pre = (grad_hidden * gelu_slope(pre_act)).astype(jnp.bfloat16)
    grad_att_rows = jnp.dot(grad_rows, dense_block.T, preferred_element_type=jnp.float32).astype(
        jnp.bfloat16
    )
    grad_att = lax.all_to_all(
        grad_att_rows, "col", split_axis=0, concat_axis=1, tiled=True
    ).reshape(four_shape)
    probability = jnp.exp(scores - totals)
    grad_probs = jnp.einsum("pihd,pjhd->phij", grad_att, values, preferred_element_type=jnp.float32)
    row_dot = jnp.sum(probability * grad_probs, axis=-1, keepdims=True)
    grad_scores = (probability * (grad_probs - row_dot) * score_scale).astype(jnp.bfloat16)
    grad_query = jnp.einsum(
        "phij,pjhd->pihd", grad_scores, key_rows, preferred_element_type=jnp.float32
    )
    grad_key = jnp.einsum(
        "phij,pihd->pjhd", grad_scores, queries, preferred_element_type=jnp.float32
    )
    grad_values = jnp.einsum(
        "phij,pihd->pjhd", weights, grad_att, preferred_element_type=jnp.float32
    )
    grad_query = unrotate(
        grad_query.reshape(own_rows, HEADS, head_dim), cosine, sine_table, ROT
    ).astype(jnp.bfloat16)
    grad_key = unrotate(
        grad_key.reshape(own_rows, HEADS, head_dim), cosine, sine_table, ROT
    ).astype(jnp.bfloat16)
    grad_values = grad_values.astype(jnp.bfloat16).reshape(own_rows, HEADS, head_dim)
    grad_mixed = jnp.stack([grad_query, grad_key, grad_values], axis=1).reshape(own_rows, 3 * width)
    grad_mixed_rows = lax.all_to_all(grad_mixed, "col", split_axis=1, concat_axis=0, tiled=True)
    grad_qkv_w = lax.dot_general(
        first_rows, grad_mixed_rows, contract_rows, preferred_element_type=jnp.float32
    )
    grad_in_w = lax.dot_general(
        second_rows, grad_pre, contract_rows, preferred_element_type=jnp.float32
    )
    qkv_weight_grad, fc_in_weight_grad = (
        lax.psum_scatter(grad_qkv_w, "row", scatter_dimension=0, tiled=True),
        lax.psum_scatter(grad_in_w, "row", scatter_dimension=0, tiled=True),
    )
    grad_dense_w = lax.dot_general(
        attended_rows, grad_rows, contract_rows, preferred_element_type=jnp.float32
    )
    grad_out_w = lax.dot_general(
        hidden, grad_rows, contract_rows, preferred_element_type=jnp.float32
    )
    dense_weight_grad, fc_out_weight_grad = (
        lax.psum_scatter(grad_dense_w, "row", scatter_dimension=1, tiled=True),
        lax.psum_scatter(grad_out_w, "row", scatter_dimension=1, tiled=True),
    )
    back_first_rows = jnp.dot(grad_mixed_rows, qkv_block.T, preferred_element_type=jnp.float32)
    back_second_rows = jnp.dot(grad_pre, fc_in_block.T, preferred_element_type=jnp.float32)
    back_first, back_second = (
        lax.psum_scatter(back_first_rows, "col", scatter_dimension=0, tiled=True),
        lax.psum_scatter(back_second_rows, "col", scatter_dimension=0, tiled=True),
    )
    input_grad = (
        grad_out.astype(jnp.float32)
        + norm_back(back_first, norm1_gain, standard, inverse)
        + norm_back(back_second, norm2_gain, standard, inverse)
    )
    norm_sums = (
        jnp.sum(back_first * standard, axis=0),
        jnp.sum(back_first, axis=0),
        jnp.sum(back_second * standard, axis=0),
        jnp.sum(back_second, axis=0),
    )
    qkv_cols = grad_mixed_rows.shape[1]
    ff_cols = grad_pre.shape[1]
    column_mask = (jnp.arange(groups, dtype=jnp.int32) == col_index)[:, None]
    qkv_bias_part = jnp.sum(grad_mixed_rows, axis=0, dtype=jnp.float32)
    in_bias_part = jnp.sum(grad_pre, axis=0, dtype=jnp.float32)
    spread_qkv = jnp.where(column_mask, qkv_bias_part[None, :], 0.0).reshape(-1)
    spread_in = jnp.where(column_mask, in_bias_part[None, :], 0.0).reshape(-1)
    gain_one, bias_one, gain_two, bias_two, out_bias, total_qkv, total_in = lax.psum(
        (
            norm_sums[0],
            norm_sums[1],
            norm_sums[2],
            norm_sums[3],
            jnp.sum(grad_out, axis=0, dtype=jnp.float32),
            spread_qkv,
            spread_in,
        ),
        ("row", "col"),
    )
    qkv_bias_grad = lax.dynamic_slice_in_dim(total_qkv, col_index * qkv_cols, qkv_cols, 0)
    fc_in_bias_grad = lax.dynamic_slice_in_dim(total_in, col_index * ff_cols, ff_cols, 0)
    return (
        block_out,
        input_grad,
        gain_one,
        bias_one,
        gain_two,
        bias_two,
        qkv_weight_grad,
        qkv_bias_grad,
        dense_weight_grad,
        out_bias,
        fc_in_weight_grad,
        fc_in_bias_grad,
        fc_out_weight_grad,
        out_bias,
    )


def solution(mesh):
    return jax.shard_map(
        on_device,
        mesh=mesh,
        in_specs=(
            P(("row", "col"), None),
            P(("row", "col"), None),
            P(("row", "col")),
            P(("row", "col")),
            P(),
            P(),
            P(),
            P(),
            P("row", "col"),
            P("col"),
            P("col", "row"),
            P(),
            P("row", "col"),
            P("col"),
            P("col", "row"),
            P(),
        ),
        out_specs=(
            P(("row", "col"), None),
            P(("row", "col"), None),
            P(),
            P(),
            P(),
            P(),
            P("row", "col"),
            P("col"),
            P("col", "row"),
            P(),
            P("row", "col"),
            P("col"),
            P("col", "row"),
            P(),
        ),
        check_vma=False,
    )
```

profile of v0, /device:TPU:0, one launch (start us, length us, event | category | flops | bytes accessed | tf_op | source)
XLA Modules:
  0.0 555.2 jit_solution(1927547153196983552)
XLA Ops:
  7.3 1.2 convert_reduce_fusion.2
  8.4 1.2 fusion.50
  9.7 2.2 fusion.38
  13.5 0.7 compare_bitcast_fusion
  14.2 1.5 convert_reduce_fusion.3
  15.7 12.3 %all_gather.22 = bf16[768,576]{1,0:T(8,128)(2,1)S(1)} all-gather(bf16[96,576]{1,0:T(8,128)(2,1)S(1)} %copy-done.18), channel_id=1, replica_groups=mesh['row'=8,'col'=4] {'row'}, dimensions={0}, use_global_device_ids=true | all-gather | bytes 995328 | tf_op jit(solution)/shard_map/all_gather | solution.py:132
  28.0 23.8 %all-gather.6.cloned.1.call-done = bf16[1024,768]{1,0:T(8,128)(2,1)} async-done(((bf16[256,768]{1,0:T(8,128)(2,1)}), bf16[1024,768]{1,0:T(8,128)(2,1)}) %all-gather.6.cloned.1.call-update) | async-done | bytes 1572880 | tf_op jit(solution)/shard_map/all_gather | solution.py:128
  51.8 2.5 add_convert_fusion.1
  54.4 1.1 copy.65
  55.5 3.5 all-to-all-start
  61.5 1.3 fusion.72
  63.2 23.8 %all-to-all-done = bf16[4,256,576]{1,2,0:T(8,128)(2,1)S(1)} async-done(((bf16[4,256,576]{1,2,0:T(8,128)(2,1)}), bf16[4,256,576]{1,2,0:T(8,128)(2,1)S(1)}, u32[]{:S(2)}, u32[]{:S(2)}) %all-to-all-start) | async-done | bytes 1179680 | tf_op jit(solution)/shard_map/all_to_all | solution.py:140
  89.5 1.6 convolution_convert_fusion.2
  91.2 3.5 all-to-all-start.1
  94.7 29.5 %all-gather.8.cloned.1.call-done = bf16[1024,768]{1,0:T(8,128)(2,1)} async-done(((bf16[256,768]{1,0:T(8,128)(2,1)}), bf16[1024,768]{1,0:T(8,128)(2,1)}) %all-gather.8.cloned.1.call-update) | async-done | bytes 1572880 | tf_op jit(solution)/shard_map/all_gather | solution.py:129
  124.2 5.4 multiply_convert_fusion.1
  129.6 31.8 %all-gather.14.cloned.1.call-done = bf16[1024,768]{1,0:T(8,128)(2,1)} async-done(((bf16[256,768]{1,0:T(8,128)(2,1)}), bf16[1024,768]{1,0:T(8,128)(2,1)}) %all-gather.14.cloned.1.call-update) | async-done | bytes 1572880 | tf_op jit(solution)/shard_map/all_gather | solution.py:171
  161.4 3.1 convolution_bitcast_fusion
  164.6 21.3 %all-gather.12.cloned.1.call-done = bf16[768,768]{0,1:T(8,128)(2,1)} async-done(((bf16[768,96]{0,1:T(8,128)(2,1)}), bf16[768,768]{0,1:T(8,128)(2,1)}) %all-gather.12.cloned.1.call-update) | async-done | bytes 1179664 | tf_op jit(solution)/shard_map/all_gather | solution.py:135
  186.0 4.7 convert_reduce_fusion
  190.7 1.2 copy-done.41
  191.9 3.1 fusion.99
  196.5 9.5 %all_gather.23 = bf16[192,768]{0,1:T(8,128)(2,1)S(1)} all-gather(bf16[192,96]{0,1:T(8,128)(2,1)} %copy.47), channel_id=1, replica_groups=mesh['row'=8,'col'=4] {'row'}, dimensions={1}, use_global_device_ids=true | all-gather | bytes 331776 | tf_op jit(solution)/shard_map/all_gather | solution.py:134
  206.7 16.6 %all_to_all.70 = bf16[4,256,192]{1,2,0:T(8,128)(2,1)S(1)} all-to-all(bf16[4,256,192]{1,2,0:T(8,128)(2,1)S(1)} %bitcast.111), channel_id=1, replica_groups=mesh['row'=8,'col'=4] {'col'}, dimensions={0} | all-to-all | bytes 786432 | tf_op jit(solution)/shard_map/all_to_all | solution.py:177
  223.3 0.8 copy-done.5
  224.1 2.3 fusion.53
  226.4 7.0 %fusion.19 = f32[256,12,64]{0,2,1:T(8,128)S(1)} fusion(f32[12,256,256]{1,2,0:T(8,128)} %fusion.53, f32[12,256,256]{1,2,0:T(8,128)} %copy-done.3, f32[12,256]{1,0:T(8,128)} %copy-done.29, pred[256,256]{0,1:T(8,128)(4,1)} %copy-done.14, bf16[256,12,48]{0,2,1:T(8,128)(2,1)} %copy-done.11, bf16[256,12,16]{0,2,1:T(8,128)(2,1)} %copy-done.20), kind=kOutput, calls=%fused_computation.25 | convolution fusion | flops 110103808 | bytes 7548928 | tf_op jit(solution)/shard_map/phij,pjhd->pihd/dot_general | solution.py:184
  233.4 7.8 %fusion.22 = f32[256,12,64]{0,2,1:T(8,128)} fusion(f32[12,256,256]{1,2,0:T(8,128)} %fusion.53, f32[12,256,256]{1,2,0:T(8,128)} %copy-done.3, f32[12,256]{1,0:T(8,128)S(1)} %copy-done.30, pred[256,256]{0,1:T(8,128)(4,1)} %copy-done.14, bf16[256,12,48]{0,2,1:T(8,128)(2,1)S(1)} %copy-done.13, bf16[256,12,16]{0,2,1:T(8,128)(2,1)} %copy-done.19), kind=kOutput, calls=%fused_computation.26 | convolution fusion | flops 110103808 | bytes 7548928 | tf_op jit(solution)/shard_map/phij,pihd->pjhd/dot_general | solution.py:187
  241.3 1.1 slice_multiply_fusion.3
  242.4 1.0 fusion.67
  243.4 1.1 fusion.55
  244.6 0.8 fusion.25
  245.6 61.8 %all_to_all.71 = bf16[256,4,576]{0,2,1:T(8,128)(2,1)S(1)} all-to-all(bf16[256,4,576]{0,2,1:T(8,128)(2,1)S(1)} %bitcast.104), channel_id=1, replica_groups=mesh['row'=8,'col'=4] {'col'}, dimensions={1} | all-to-all | bytes 2359296 | tf_op jit(solution)/shard_map/all_to_all | solution.py:201
  307.5 1.0 copy-done.7
  308.6 3.2 fusion.98
  311.8 3.2 fusion.97
  315.0 1.8 add_convert_fusion
  316.9 4.8 fusion.101
  321.7 4.3 fusion.102
  326.4 4.6 fusion.100
  331.2 1.8 copy.58
  333.4 40.4 %reduce-scatter.12.cloned.1.call-done = f32[256,768]{1,0:T(8,128)} async-done(((f32[1024,768]{1,0:T(8,128)}), f32[256,768]{1,0:T(8,128)}) %reduce-scatter.12.cloned.1.call-update) | async-done | bytes 786448 | tf_op jit(solution)/shard_map/reduce_scatter | solution.py:225
  373.8 2.1 fusion.48
  375.8 43.6 %all-reduce = (f32[768]{0:T(1024)}, f32[768]{0:T(1024)}, f32[768]{0:T(1024)}, f32[768]{0:T(1024)}, f32[2304]{0:T(1024)S(1)}, /*index=5*/f32[768]{0:T(1024)S(1)}, f32[3072]{0:T(1024)S(1)}) all-reduce(f32[768]{0:T(1024)S(1)} %get-tuple-element.16, f32[768]{0:T(1024)S(1)} %get-tuple-element.21, ...), channel_id=1, replica_groups=mesh['row'=8,'col'=4] {'row','col'}, use_global_device_ids=true, to_apply=%region_13.14 | all-reduce | flops 9216 | bytes 73728 | tf_op jit(solution)/shard_map/psum | solution.py:246
  420.9 3.2 fusion.47
  424.1 33.4 %reduce-scatter.18.cloned.1.call-done = f32[96,768]{1,0:T(8,128)} async-done(((f32[768,768]{1,0:T(8,128)}), f32[96,768]{1,0:T(8,128)}) %reduce-scatter.18.cloned.1.call-update) | async-done | bytes 294928 | tf_op jit(solution)/shard_map/reduce_scatter | solution.py:210
  457.5 46.3 %reduce-scatter.20.cloned.1.call-done = f32[768,96]{0,1:T(8,128)} async-done(((f32[768,768]{0,1:T(8,128)}), f32[768,96]{0,1:T(8,128)}) %reduce-scatter.20.cloned.1.call-update) | async-done | bytes 294928 | tf_op jit(solution)/shard_map/reduce_scatter | solution.py:220
  503.8 44.0 %reduce-scatter.16.cloned.1.call-done = f32[96,576]{1,0:T(8,128)} async-done(((f32[768,576]{1,0:T(8,128)}), f32[96,576]{1,0:T(8,128)}) %reduce-scatter.16.cloned.1.call-update) | async-done | bytes 221200 | tf_op jit(solution)/shard_map/reduce_scatter | solution.py:209
  (150 shorter events, 11.9 us)
Async XLA Ops:
  7.2 7.0 %copy-start.10 = (bf16[256,768]{1,0:T(8,128)(2,1)S(1)}, bf16[256,768]{1,0:T(8,128)(2,1)}, u32[]{:S(2)}) copy-start(bf16[256,768]{1,0:T(8,128)(2,1)} %param.17) | copy-start | bytes 1179652
  7.2 8.5 %copy-start.18 = (bf16[96,576]{1,0:T(8,128)(2,1)S(1)}, bf16[96,576]{1,0:T(8,128)(2,1)}, u32[]{:S(2)}) copy-start(bf16[96,576]{1,0:T(8,128)(2,1)} %param.24) | copy-start | bytes 331780
  7.2 44.6 %copy-start.38 = (f32[576]{0:T(1024)S(1)}, f32[576]{0:T(1024)}, u32[]{:S(2)}) copy-start(f32[576]{0:T(1024)} %param.25) | copy-start | bytes 6916
  7.2 44.6 %all-gather.6.cloned.1.call-start = ((), (), s32[]{:S(2)}) async-start(), calls=%async_computation.11 | async-start | bytes 1966080 | tf_op jit(solution)/shard_map/all_gather | solution.py:128
  8.4 7.3 %copy-start.24 = (f32[256]{0:T(256)}, f32[256]{0:T(256)S(1)}, u32[]{:S(2)}) copy-start(f32[256]{0:T(256)S(1)} %broadcast_multiply_fusion.5) | copy-start | bytes 3076
  9.7 6.0 %copy-start.26 = (f32[256]{0:T(256)}, f32[256]{0:T(256)S(1)}, u32[]{:S(2)}) copy-start(f32[256]{0:T(256)S(1)} %add_rsqrt_fusion) | copy-start | bytes 3076
  11.9 82.8 %all-gather.10.cloned.1.call-start = ((), (), s32[]{:S(2)}) async-start(), calls=%async_computation.13 | async-start | bytes 1327104 | tf_op jit(solution)/shard_map/all_gather | solution.py:133
  12.7 111.5 %all-gather.8.cloned.1.call-start = ((), (), s32[]{:S(2)}) async-start(), calls=%async_computation.12 | async-start | bytes 1966080 | tf_op jit(solution)/shard_map/all_gather | solution.py:129
  13.4 148.0 %all-gather.14.cloned.1.call-start = ((), (), s32[]{:S(2)}) async-start(), calls=%async_computation.16 | async-start | bytes 1966080 | tf_op jit(solution)/shard_map/all_gather | solution.py:171
  28.0 26.4 %copy-start.8 = (bf16[768,576]{1,0:T(8,128)(2,1)}, bf16[768,576]{1,0:T(8,128)(2,1)S(1)}, u32[]{:S(2)}) copy-start(bf16[768,576]{1,0:T(8,128)(2,1)S(1)} %all_gather.22) | copy-start | bytes 2654212
  54.4 5.3 copy-start.40
  54.4 6.5 %copy-start.36 = (s32[2]{0:T(128)S(1)}, s32[2]{0:T(128)}, u32[]{:S(2)}) copy-start(s32[2]{0:T(128)} %param.18) | copy-start | bytes 28
  55.5 31.4 %all-to-all-start = ((bf16[4,256,576]{1,2,0:T(8,128)(2,1)}), bf16[4,256,576]{1,2,0:T(8,128)(2,1)S(1)}, u32[]{:S(2)}, u32[]{:S(2)}) async-start(bf16[4,256,576]{1,2,0:T(8,128)(2,1)} %bitcast.101), calls=%async_computation | async-start | bytes 2359296 | tf_op jit(solution)/shard_map/all_to_all | solution.py:140
  59.1 126.9 %all-gather.12.cloned.1.call-start = ((), (), s32[]{:S(2)}) async-start(), calls=%async_computation.14 | async-start | bytes 1327104 | tf_op jit(solution)/shard_map/all_gather | solution.py:135
  63.0 25.8 %copy-start.16 = (f32[256,16]{0,1:T(8,128)}, f32[256,16]{0,1:T(8,128)S(1)}, u32[]{:S(2)}) copy-start(f32[256,16]{0,1:T(8,128)S(1)} %get-tuple-element.58) | copy-start | bytes 49156
  63.2 26.4 %copy-start.14 = (pred[256,256]{0,1:T(8,128)(4,1)}, pred[256,256]{0,1:T(8,128)(4,1)S(1)}, u32[]{:S(2)}) copy-start(pred[256,256]{0,1:T(8,128)(4,1)S(1)} %fusion.57) | copy-start | bytes 196612
  87.3 2.2 copy-start.19
  88.8 2.4 copy-start.3
  89.5 34.7 %copy-start.39 = (f32[768]{0:T(1024)S(1)}, f32[768]{0:T(1024)}, u32[]{:S(2)}) copy-start(f32[768]{0:T(1024)} %param.29) | copy-start | bytes 9220
  91.2 38.4 %all-to-all-start.1 = ((bf16[256,4,192]{0,2,1:T(8,128)(2,1)}), bf16[256,4,192]{0,2,1:T(8,128)(2,1)S(1)}, u32[]{:S(2)}, u32[]{:S(2)}) async-start(bf16[256,4,192]{0,2,1:T(8,128)(2,1)} %bitcast.14), calls=%async_computation.1 | async-start | bytes 786432 | tf_op jit(solution)/shard_map/all_to_all | solution.py:157
  94.6 236.6 %reduce-scatter.22.cloned.1.call-start = ((), (), s32[]{:S(2)}) async-start(), calls=%async_computation.22 | async-start | bytes 884736
  161.4 24.5 %copy-start.1 = (bf16[1024,768]{1,0:T(8,128)(2,1)S(1)}, bf16[1024,768]{1,0:T(8,128)(2,1)}, u32[]{:S(2)}) copy-start(bf16[1024,768]{1,0:T(8,128)(2,1)} %all-gather.14.cloned.1.call-done) | copy-start | bytes 4718596
  164.6 168.8 %reduce-scatter.14.cloned.1.call-start = ((), (), s32[]{:S(2)}) async-start(), calls=%async_computation.18 | async-start | bytes 3932160 | tf_op jit(solution)/shard_map/reduce_scatter | solution.py:226
  186.0 5.9 %copy-start.37 = (bf16[768,768]{1,0:T(8,128)(2,1)S(1)}, bf16[768,768]{1,0:T(8,128)(2,1)}, u32[]{:S(2)}) copy-start(bf16[768,768]{1,0:T(8,128)(2,1)} %all-gather.10.cloned.1.call-done) | copy-start | bytes 3538948
  195.0 178.8 %reduce-scatter.12.cloned.1.call-start = ((), (), s32[]{:S(2)}) async-start(), calls=%async_computation.17 | async-start | bytes 3932160 | tf_op jit(solution)/shard_map/reduce_scatter | solution.py:225
  226.4 7.0 %copy-start.13 = (bf16[256,12,48]{0,2,1:T(8,128)(2,1)S(1)}, bf16[256,12,48]{0,2,1:T(8,128)(2,1)}, u32[]{:S(2)}) copy-start(bf16[256,12,48]{0,2,1:T(8,128)(2,1)} %copy-done.12) | copy-start | bytes 884740
  226.4 7.0 %copy-start.30 = (f32[12,256]{1,0:T(8,128)S(1)}, f32[12,256]{1,0:T(8,128)}, u32[]{:S(2)}) copy-start(f32[12,256]{1,0:T(8,128)} %copy-done.29) | copy-start | bytes 36868
  233.4 7.9 %copy-start.17 = (f32[256,16]{0,1:T(8,128)S(1)}, f32[256,16]{0,1:T(8,128)}, u32[]{:S(2)}) copy-start(f32[256,16]{0,1:T(8,128)} %copy-done.16) | copy-start | bytes 49156
  241.3 3.3 copy-start.4
  241.3 3.4 copy-start.6
  241.3 3.4 copy-start.15
  241.3 3.4 copy-start.31
  245.5 63.1 %copy-start.9 = (bf16[768,576]{1,0:T(8,128)(2,1)S(1)}, bf16[768,576]{1,0:T(8,128)(2,1)}, u32[]{:S(2)}) copy-start(bf16[768,576]{1,0:T(8,128)(2,1)} %copy-done.8) | copy-start | bytes 2654212
  311.8 109.1 %reduce-scatter.10.cloned.1.call-start = ((), (), s32[]{:S(2)}) async-start(), calls=%async_computation.15 | async-start | bytes 1966080 | tf_op jit(solution)/shard_map/reduce_scatter | solution.py:160
  316.8 140.7 %reduce-scatter.18.cloned.1.call-start = ((), (), s32[]{:S(2)}) async-start(), calls=%async_computation.20 | async-start | bytes 2654208 | tf_op jit(solution)/shard_map/reduce_scatter | solution.py:210
  321.7 182.1 %reduce-scatter.20.cloned.1.call-start = ((), (), s32[]{:S(2)}) async-start(), calls=%async_computation.21 | async-start | bytes 2654208 | tf_op jit(solution)/shard_map/reduce_scatter | solution.py:220
  326.1 5.0 copy-start.35
  326.1 221.7 %reduce-scatter.16.cloned.1.call-start = ((), (), s32[]{:S(2)}) async-start(), calls=%async_computation.19 | async-start | bytes 2211840 | tf_op jit(solution)/shard_map/reduce_scatter | solution.py:209
  331.0 42.8 %copy-start = (bf16[256,768]{1,0:T(8,128)(2,1)S(1)}, bf16[256,768]{1,0:T(8,128)(2,1)}, u32[]{:S(2)}) copy-start(bf16[256,768]{1,0:T(8,128)(2,1)} %param.16) | copy-start | bytes 1179652
  331.0 42.8 %copy-start.22 = (f32[768]{0:T(1024)S(1)}, f32[768]{0:T(1024)}, u32[]{:S(2)}) copy-start(f32[768]{0:T(1024)} %param.20) | copy-start | bytes 9220
  331.0 42.8 %copy-start.23 = (f32[768]{0:T(1024)S(1)}, f32[768]{0:T(1024)}, u32[]{:S(2)}) copy-start(f32[768]{0:T(1024)} %param.22) | copy-start | bytes 9220
  331.0 42.8 %copy-start.25 = (f32[256]{0:T(256)S(1)}, f32[256]{0:T(256)}, u32[]{:S(2)}) copy-start(f32[256]{0:T(256)} %copy-done.24) | copy-start | bytes 3076
  331.0 42.8 %copy-start.27 = (f32[256]{0:T(256)S(1)}, f32[256]{0:T(256)}, u32[]{:S(2)}) copy-start(f32[256]{0:T(256)} %copy-done.26) | copy-start | bytes 3076
  331.0 44.8 %copy-start.28 = (f32[768]{0:T(1024)S(1)}, f32[768]{0:T(1024)}, u32[]{:S(2)}) copy-start(f32[768]{0:T(1024)} %get-tuple-element.33) | copy-start | bytes 9220
  331.0 89.9 %copy-start.2 = (bf16[256,768]{1,0:T(8,128)(2,1)S(1)}, bf16[256,768]{1,0:T(8,128)(2,1)}, u32[]{:S(2)}) copy-start(bf16[256,768]{1,0:T(8,128)(2,1)} %get-tuple-element.34) | copy-start | bytes 1179652
  331.0 89.9 %copy-start.32 = (f32[768]{0:T(1024)S(1)}, f32[768]{0:T(1024)}, u32[]{:S(2)}) copy-start(f32[768]{0:T(1024)} %param.31) | copy-start | bytes 9220
  331.0 89.9 %copy-start.33 = (f32[768]{0:T(1024)S(1)}, f32[768]{0:T(1024)}, u32[]{:S(2)}) copy-start(f32[768]{0:T(1024)} %param.27) | copy-start | bytes 9220
  419.5 128.9 %copy-start.34 = (f32[768]{0:T(1024)}, f32[768]{0:T(1024)S(1)}, u32[]{:S(2)}) copy-start(f32[768]{0:T(1024)S(1)} %get-tuple-element.96) | copy-start | bytes 9220
  (8 other events, 9.7 us)
Sparse Core Ops, SparseCore 0:
  12.1 39.7 all-gather.5
  53.7 22.7 all-gather.9
  78.7 45.4 all-gather.7
  125.6 35.8 all-gather.13
  163.2 22.7 all-gather.11
  189.6 34.9 reduce-scatter.21
  226.8 79.1 reduce-scatter.13
  311.9 61.8 reduce-scatter.11
  376.0 36.3 reduce-scatter.9
  416.2 41.1 reduce-scatter.17
  461.4 42.3 reduce-scatter.19
  507.6 40.1 reduce-scatter.15
where the time goes:
time: 556 us; the launch traced here: 555 us
  waiting for transfers between devices  296 us (53%)
  blocking collectives  144 us (26%)
  matrix products  61.7 us (11%)
  other arithmetic  17.4 us (3%)
  between operations  15.5 us (3%)
  local copies, waits for them, and re-layouts  12.7 us (2%)
  starting transfers between devices  7.7 us (1%)
    all_to_all x1, blocking collectives, on_device(): lax.all_to_all(grad_mixed, 'col', split_axis=1, concat_axis=0, tiled=True)  61.8 us
    reduce_scatter x1, waiting for transfers between devices, on_device(): lax.psum_scatter(grad_out_w, 'row', scatter_dimension=1, tiled=True)  46.3 us
    reduce_scatter x1, waiting for transfers between devices, on_device(): lax.psum_scatter(grad_qkv_w, 'row', scatter_dimension=0, tiled=True)  44 us
    psum x1, blocking collectives, on_device(): lax.psum((norm_sums[0], norm_sums[1], norm_sums[2], norm_sums[3], jnp.sum...  43.6 us
    reduce_scatter x1, waiting for transfers between devices, on_device(): lax.psum_scatter(back_first_rows, 'col', scatter_dimension=0, tiled=True)  40.4 us
    reduce_scatter x1, waiting for transfers between devices, on_device(): lax.psum_scatter(grad_in_w, 'row', scatter_dimension=0, tiled=True)  33.4 us
    all_gather x1, waiting for transfers between devices, on_device(): grad_rows = lax.all_gather(grad_out, 'col', axis=0, tiled=True)  31.8 us
    all_gather x1, waiting for transfers between devices, on_device(): lax.all_gather(normed_second, 'col', axis=0, tiled=True)  29.5 us
  transfers between devices with their start and end apart: 14, of which 9 were waited for; matrix products, arithmetic and copies ran while one was open for 15% of the time, Pallas kernels for 0%

commit v1 on v0

v1 whole, which is shorter than its diff:
```python
import math

import jax
import jax.numpy as jnp
from jax import lax
from jax.experimental import pallas as pl
from jax.experimental.pallas import tpu as pltpu
from jax.sharding import PartitionSpec as P

HEADS = 12
ROT = 16


NORM_EPSILON = 1e-05
HALF_ROOT = math.sqrt(0.5)
DENSITY_SCALE = 1.0 / math.sqrt(2.0 * math.pi)


def normalize(features):
    widened = features.astype(jnp.float32)
    centered = widened - jnp.mean(widened, axis=1, keepdims=True)
    inverse = lax.rsqrt(jnp.mean(centered * centered, axis=1, keepdims=True) + NORM_EPSILON)
    return (centered * inverse, inverse)


def norm_back(grad_normed, gain, standard, inverse):
    grad_unit = grad_normed * gain
    return inverse * (
        grad_unit
        - jnp.mean(grad_unit, axis=1, keepdims=True)
        - standard * jnp.mean(grad_unit * standard, axis=1, keepdims=True)
    )


def gelu_exact(pre_act):
    return 0.5 * pre_act * (1.0 + lax.erf(pre_act * HALF_ROOT))


def gelu_slope(pre_act):
    return (
        0.5 * (1.0 + lax.erf(pre_act * HALF_ROOT))
        + pre_act * jnp.exp(-0.5 * pre_act * pre_act) * DENSITY_SCALE
    )


def rotary_tables(positions, rotated):
    halves = rotated // 2
    frequency = 10000.0 ** (-2.0 * jnp.arange(halves, dtype=jnp.float32) / rotated)
    angles = positions[:, None].astype(jnp.float32) * frequency[None, :]
    angles = jnp.concatenate([angles, angles], axis=1)
    return (jnp.cos(angles)[:, None, :], jnp.sin(angles)[:, None, :])


def rotate(values, cosine, sine_table, rotated):
    halves = rotated // 2
    leading = values[..., :rotated]
    turned = jnp.concatenate([-leading[..., halves:], leading[..., :halves]], axis=-1)
    return jnp.concatenate([leading * cosine + turned * sine_table, values[..., rotated:]], axis=-1)


def unrotate(gradient, cosine, sine_table, rotated):
    halves = rotated // 2
    leading = gradient[..., :rotated]
    scaled = leading * sine_table
    turned = jnp.concatenate([scaled[..., halves:], -scaled[..., :halves]], axis=-1)
    return jnp.concatenate([leading * cosine + turned, gradient[..., rotated:]], axis=-1)


def pair_mask(lengths, offsets, block_rows):
    pair_count = lengths.shape[0] // 2
    local_rows = jnp.arange(2 * block_rows, dtype=jnp.int32)
    block_of = local_rows // block_rows
    in_block = local_rows % block_rows
    pair_lengths = lengths.reshape(pair_count, 2)
    joined = offsets.reshape(pair_count, 2)[:, 1] > 0
    row_limit = jnp.where(block_of[None, :] == 0, pair_lengths[:, 0:1], pair_lengths[:, 1:2])
    live_keys = in_block[None, :] < row_limit
    same_seq = (block_of[:, None] == block_of[None, :])[None, :, :] | joined[:, None, None]
    causal = (local_rows[None, :] <= local_rows[:, None])[None, :, :]
    diagonal = (local_rows[:, None] == local_rows[None, :])[None, :, :]
    return same_seq & causal & (live_keys[:, None, :] | diagonal)


def masked_scores(queries, key_rows, allowed, score_scale):
    scores = (
        jnp.einsum("pihd,pjhd->phij", queries, key_rows, preferred_element_type=jnp.float32)
        * score_scale
    )
    return jnp.where(allowed[:, None, :, :], scores, -jnp.inf)


MESH = pl.DeviceIdType.MESH
RING_ROWS = 8
RING_COLS = 4


def partners():
    row = lax.axis_index("row")
    col = lax.axis_index("col")
    beside = row + 1 - 2 * (row % 2)
    across = row + 2 - 4 * ((row // 2) % 2)
    above = row + 4 - 8 * (row // 4)
    return row, col, beside, across, above


def greet(row, col, beside, across, above):
    barrier = pltpu.get_barrier_semaphore()
    others = [(beside, col), (across, col), (above, col)]
    others += [(row, (col + step) % RING_COLS) for step in range(1, RING_COLS)]
    for other in others:
        pl.semaphore_signal(barrier, inc=1, device_id=other, device_id_type=MESH)
    pl.semaphore_wait(barrier, len(others))


class Sends:
    def __init__(self, send_sems, recv_sems):
        self.send_sems = send_sems
        self.recv_sems = recv_sems
        self.copies = {}

    def start(self, name, source, target, device):
        at = len(self.copies)
        copy = pltpu.make_async_remote_copy(
            src_ref=source,
            dst_ref=target,
            send_sem=self.send_sems.at[at],
            recv_sem=self.recv_sems.at[at],
            device_id=device,
            device_id_type=MESH,
        )
        copy.start()
        self.copies[name] = copy

    def arrived(self, name):
        self.copies[name].wait_recv()

    def finish(self):
        for copy in self.copies.values():
            copy.wait_send()


GATHER_COPIES = 39


def gather_kernel(shard, out, own_sem, send_sems, recv_sems):
    row, col, beside, across, above = partners()
    diagonal = across + 4 - 8 * (across // 4)
    half = shard.shape[0] // 2
    low, high = pl.ds(0, half), pl.ds(half, half)
    greet(row, col, beside, across, above)
    sends = Sends(send_sems, recv_sems)
    own = pltpu.make_async_copy(shard, out.at[col, row], own_sem)
    own.start()

    def share(step):
        at = (col - step + RING_COLS) % RING_COLS
        piece = shard if step == 0 else out.at[at, row]
        sends.start(("x", step), piece, out.at[at, row], (across, col))
        sends.start(("y", step), piece, out.at[at, row], (above, col))
        if step == 0:
            for hop in (1, 2, 3):
                there = (col + hop) % RING_COLS
                sends.start(("z", hop), shard, out.at[col, row], (row, there))
        sends.start(("c", step), piece, out.at[at, row], (beside, col))

    def relay(step):
        at = (col - step + RING_COLS) % RING_COLS
        sends.arrived(("x", step))
        sends.start(("dy", step), out.at[at, across, high], out.at[at, across, high], (above, col))
        sends.start(("cx", step), out.at[at, across], out.at[at, across], (beside, col))
        sends.arrived(("y", step))
        sends.start(("dx", step), out.at[at, above, low], out.at[at, above, low], (across, col))
        sends.start(("cy", step), out.at[at, above], out.at[at, above], (beside, col))

    def close(step):
        at = (col - step + RING_COLS) % RING_COLS
        sends.arrived(("dx", step))
        sends.start(("cdx", step), out.at[at, diagonal, low], out.at[at, diagonal, low], (beside, col))
        sends.arrived(("dy", step))
        sends.start(("cdy", step), out.at[at, diagonal, high], out.at[at, diagonal, high], (beside, col))

    share(0)
    sends.arrived(("z", 1))
    share(1)
    relay(0)
    sends.arrived(("z", 2))
    share(2)
    relay(1)
    close(0)
    sends.arrived(("z", 3))
    share(3)
    relay(2)
    close(1)
    relay(3)
    close(2)
    close(3)
    for step in range(RING_COLS):
        for kind in ("c", "cx", "cy", "cdx", "cdy"):
            sends.arrived((kind, step))
    sends.finish()
    own.wait()


def gather_shards(shard, rows, cols):
    if (rows, cols) != (RING_ROWS, RING_COLS):
        return lax.all_gather(shard, ("col", "row"), axis=0, tiled=True).reshape(
            cols, rows * shard.shape[0], shard.shape[1]
        )
    gathered = pl.pallas_call(
        gather_kernel,
        out_shape=jax.ShapeDtypeStruct((cols, rows) + shard.shape, shard.dtype),
        in_specs=[pl.BlockSpec(memory_space=pl.ANY)],
        out_specs=pl.BlockSpec(memory_space=pl.ANY),
        scratch_shapes=[
            pltpu.SemaphoreType.DMA,
            pltpu.SemaphoreType.DMA((GATHER_COPIES,)),
            pltpu.SemaphoreType.DMA((GATHER_COPIES,)),
        ],
        compiler_params=pltpu.CompilerParams(collective_id=0, has_side_effects=True),
    )(shard)
    return gathered.reshape(cols, rows * shard.shape[0], shard.shape[1])


SCATTER_COPIES = 40


def add_rows(target, source, start, count):
    @pl.loop(0, count // 16)
    def _(tile):
        rows = pl.ds(pl.multiple_of(start + tile * 16, 16), 16)
        target[rows, :] = (
            target[rows, :].astype(jnp.float32) + source[rows, :].astype(jnp.float32)
        ).astype(target.dtype)


SELF, ACROSS, ABOVE, DIAGONAL = range(4)


def scatter_kernel(
    grads,
    small,
    out,
    small_out,
    total,
    from_core,
    from_x,
    from_y,
    diag_x,
    diag_y,
    from_z,
    small_in,
    small_sum,
    own_sems,
    send_sems,
    recv_sems,
):
    row, col, beside, across, above = partners()
    diagonal = across + 4 - 8 * (across // 4)
    chips = (row, across, above, diagonal)
    height = out.shape[0]
    half = height // 2
    low, high = pl.ds(0, half), pl.ds(half, half)
    order = (1, 2, 3, 0)
    places = (DIAGONAL, ACROSS, ABOVE, SELF)
    greet(row, col, beside, across, above)
    sends = Sends(send_sems, recv_sems)
    next_col = col + 1 - 2 * (col % 2)
    far_col = col + 2 - 4 * (col // 2)
    small_targets = ((beside, col), (across, col), (above, col), (row, next_col), (row, far_col))

    def send_small(stage):
        sends.start(("s", stage), small_sum.at[stage], small_in.at[stage], small_targets[stage])

    def fold_small(stage):
        sends.arrived(("s", stage))
        summed = small_sum[stage] + small_in[stage]
        if stage + 1 < len(small_targets):
            small_sum[stage + 1] = summed
            send_small(stage + 1)
        else:
            small_out[...] = summed

    small_sum[0] = small[...]
    loads = {}
    for step in order:
        at = (col + step) % RING_COLS
        for place in places:
            chip = chips[place]
            other = chip + 1 - 2 * (chip % 2)
            sends.start(
                ("c", step, place), grads.at[at, other], from_core.at[step, place], (beside, col)
            )
            load = pltpu.make_async_copy(
                grads.at[at, chip], total.at[step, place], own_sems.at[step * 4 + place]
            )
            load.start()
            loads[step, place] = load
    send_small(0)

    def pair(step):
        for place in places:
            loads[step, place].wait()
            sends.arrived(("c", step, place))
            add_rows(total.at[step, place], from_core.at[step, place], 0, height)
            if place == DIAGONAL:
                sends.start(
                    ("dx", step), total.at[step, DIAGONAL, low], diag_x.at[step, low], (across, col)
                )
                sends.start(
                    ("dy", step), total.at[step, DIAGONAL, high], diag_y.at[step, high], (above, col)
                )

    def turn(step):
        sends.arrived(("dx", step))
        add_rows(total.at[step, ABOVE], diag_x.at[step], 0, half)
        sends.start(("y", step), total.at[step, ABOVE], from_y.at[step], (above, col))
        sends.arrived(("dy", step))
        add_rows(total.at[step, ACROSS], diag_y.at[step], half, half)
        sends.start(("x", step), total.at[step, ACROSS], from_x.at[step], (across, col))

    def leave(step):
        sends.arrived(("x", step))
        add_rows(total.at[step, SELF], from_x.at[step], 0, height)
        sends.arrived(("y", step))
        add_rows(total.at[step, SELF], from_y.at[step], 0, height)
        if step > 0:
            there = (col + step) % RING_COLS
            sends.start(("z", step), total.at[step, SELF], from_z.at[step - 1], (row, there))

    for turn_at in range(len(order) + 2):
        if turn_at < len(order):
            pair(order[turn_at])
        if 1 <= turn_at <= len(order):
            turn(order[turn_at - 1])
        if turn_at >= 2:
            leave(order[turn_at - 2])
        if turn_at < len(small_targets):
            fold_small(turn_at)
    for step in (1, 2, 3):
        sends.arrived(("z", step))

    @pl.loop(0, height // 16)
    def _(tile):
        rows = pl.ds(pl.multiple_of(tile * 16, 16), 16)
        out[rows, :] = (
            total[0, SELF, rows, :].astype(jnp.float32)
            + from_z[0, rows, :].astype(jnp.float32)
            + from_z[1, rows, :].astype(jnp.float32)
            + from_z[2, rows, :].astype(jnp.float32)
        )

    sends.finish()


def scatter_grads(grads, small, rows, cols):
    height, width = grads.shape[1] // rows, grads.shape[2]
    if (rows, cols) != (RING_ROWS, RING_COLS):
        flat = grads.reshape(cols * rows * height, width)
        return (
            lax.psum_scatter(flat, ("col", "row"), scatter_dimension=0, tiled=True).astype(
                jnp.float32
            ),
            lax.psum(small, ("row", "col")),
        )
    kind = grads.dtype
    shape = (height, width)
    return pl.pallas_call(
        scatter_kernel,
        out_shape=(
            jax.ShapeDtypeStruct(shape, jnp.float32),
            jax.ShapeDtypeStruct(small.shape, small.dtype),
        ),
        in_specs=[pl.BlockSpec(memory_space=pl.ANY), pl.BlockSpec(memory_space=pltpu.VMEM)],
        out_specs=(
            pl.BlockSpec(memory_space=pltpu.VMEM),
            pl.BlockSpec(memory_space=pltpu.VMEM),
        ),
        scratch_shapes=[
            pltpu.VMEM((cols, 4) + shape, kind),
            pltpu.VMEM((cols, 4) + shape, kind),
            pltpu.VMEM((cols,) + shape, kind),
            pltpu.VMEM((cols,) + shape, kind),
            pltpu.VMEM((cols,) + shape, kind),
            pltpu.VMEM((cols,) + shape, kind),
            pltpu.VMEM((cols - 1,) + shape, kind),
            pltpu.VMEM((5,) + small.shape, small.dtype),
            pltpu.VMEM((5,) + small.shape, small.dtype),
            pltpu.SemaphoreType.DMA((16,)),
            pltpu.SemaphoreType.DMA((SCATTER_COPIES,)),
            pltpu.SemaphoreType.DMA((SCATTER_COPIES,)),
        ],
        compiler_params=pltpu.CompilerParams(
            collective_id=1, has_side_effects=True, vmem_limit_bytes=56 * 2**20
        ),
    )(grads.reshape(cols, rows, height, width), small)


def on_device(
    block_input,
    block_cotangent,
    block_lengths,
    block_offsets,
    norm1_gain,
    norm1_bias,
    norm2_gain,
    norm2_bias,
    qkv_weight,
    qkv_bias,
    dense_weight,
    dense_bias,
    fc_in_weight,
    fc_in_bias,
    fc_out_weight,
    fc_out_bias,
):
    rows = lax.axis_size("row")
    cols = lax.axis_size("col")
    col_index = lax.axis_index("col")
    own_rows = block_input.shape[0]
    width = block_input.shape[1]
    head_dim = width // HEADS
    block_count = block_lengths.shape[0]
    block_rows = own_rows // block_count
    pair_count = block_count // 2
    four_shape = (pair_count, 2 * block_rows, HEADS, head_dim)
    score_scale = head_dim ** (-0.5)
    qkv_cols = qkv_weight.shape[1]
    att_cols = dense_weight.shape[0]
    ff_cols = fc_in_weight.shape[1]
    cuts = (qkv_cols, qkv_cols + att_cols, qkv_cols + att_cols + ff_cols)

    shard = jnp.concatenate([qkv_weight, dense_weight.T, fc_in_weight, fc_out_weight.T], axis=1)
    biases = lax.all_gather(jnp.concatenate([qkv_bias, fc_in_bias]), "col", axis=0, tiled=False)
    qkv_bias_full = biases[:, :qkv_cols].reshape(-1)
    fc_in_bias_full = biases[:, qkv_cols:].reshape(-1)
    gathered = gather_shards(shard, rows, cols)
    qkv_full = gathered[:, :, : cuts[0]]
    dense_full = gathered[:, :, cuts[0] : cuts[1]]
    fc_in_full = gathered[:, :, cuts[1] : cuts[2]]
    fc_out_full = gathered[:, :, cuts[2] :]

    in_block = jnp.arange(block_rows, dtype=jnp.int32)
    positions = (block_offsets[:, None] + in_block[None, :]).reshape(-1)
    valid = (in_block[None, :] < block_lengths[:, None]).reshape(-1)
    cosine, sine_table = rotary_tables(positions, ROT)
    allowed = pair_mask(block_lengths, block_offsets, block_rows)
    standard, inverse = normalize(block_input)
    normed_first = (standard * norm1_gain + norm1_bias).astype(jnp.bfloat16)
    normed_second = (standard * norm2_gain + norm2_bias).astype(jnp.bfloat16)
    grad_out = jnp.where(valid[:, None], block_cotangent, jnp.zeros_like(block_cotangent))

    def widen(left, weight):
        return jnp.einsum("rd,cdw->rcw", left, weight, preferred_element_type=jnp.float32).reshape(
            left.shape[0], -1
        )

    def narrow(left, weight):
        split = left.reshape(left.shape[0], cols, -1)
        return jnp.einsum("rcw,cdw->rd", split, weight, preferred_element_type=jnp.float32)

    def outer(left, right):
        split = right.reshape(right.shape[0], cols, -1)
        return jnp.einsum(
            "rd,rcw->cdw", left, split, preferred_element_type=jnp.float32
        ).astype(jnp.bfloat16)

    mixed = (widen(normed_first, qkv_full) + qkv_bias_full).astype(jnp.bfloat16)
    mixed = mixed.reshape(own_rows, 3, HEADS, head_dim)
    queries = rotate(mixed[:, 0].astype(jnp.float32), cosine, sine_table, ROT).astype(jnp.bfloat16)
    key_rows = rotate(mixed[:, 1].astype(jnp.float32), cosine, sine_table, ROT).astype(jnp.bfloat16)
    queries = queries.reshape(four_shape)
    key_rows = key_rows.reshape(four_shape)
    values = mixed[:, 2].reshape(four_shape)
    scores = masked_scores(queries, key_rows, allowed, score_scale)
    highest = jnp.max(scores, axis=-1, keepdims=True)
    totals = highest + jnp.log(jnp.sum(jnp.exp(scores - highest), axis=-1, keepdims=True))
    probability = jnp.exp(scores - totals)
    weights = probability.astype(jnp.bfloat16)
    attended = jnp.einsum("phij,pjhd->pihd", weights, values, preferred_element_type=jnp.float32)
    attended = attended.astype(jnp.bfloat16).reshape(own_rows, width)
    pre_act = widen(normed_second, fc_in_full) + fc_in_bias_full
    hidden = gelu_exact(pre_act).astype(jnp.bfloat16)
    summed = narrow(attended, dense_full) + narrow(hidden, fc_out_full)
    block_out = block_input.astype(jnp.float32) + dense_bias + fc_out_bias + summed
    grad_pre = (widen(grad_out, fc_out_full) * gelu_slope(pre_act)).astype(jnp.bfloat16)
    grad_att = widen(grad_out, dense_full).astype(jnp.bfloat16).reshape(four_shape)
    grad_probs = jnp.einsum("pihd,pjhd->phij", grad_att, values, preferred_element_type=jnp.float32)
    row_dot = jnp.sum(probability * grad_probs, axis=-1, keepdims=True)
    grad_scores = (probability * (grad_probs - row_dot) * score_scale).astype(jnp.bfloat16)
    grad_query = jnp.einsum(
        "phij,pjhd->pihd", grad_scores, key_rows, preferred_element_type=jnp.float32
    )
    grad_key = jnp.einsum(
        "phij,pihd->pjhd", grad_scores, queries, preferred_element_type=jnp.float32
    )
    grad_values = jnp.einsum(
        "phij,pihd->pjhd", weights, grad_att, preferred_element_type=jnp.float32
    )
    grad_query = unrotate(
        grad_query.reshape(own_rows, HEADS, head_dim), cosine, sine_table, ROT
    ).astype(jnp.bfloat16)
    grad_key = unrotate(
        grad_key.reshape(own_rows, HEADS, head_dim), cosine, sine_table, ROT
    ).astype(jnp.bfloat16)
    grad_values = grad_values.astype(jnp.bfloat16).reshape(own_rows, HEADS, head_dim)
    grad_mixed = jnp.stack([grad_query, grad_key, grad_values], axis=1).reshape(own_rows, 3 * width)
    back_first = narrow(grad_mixed, qkv_full)
    back_second = narrow(grad_pre, fc_in_full)
    input_grad = (
        grad_out.astype(jnp.float32)
        + norm_back(back_first, norm1_gain, standard, inverse)
        + norm_back(back_second, norm2_gain, standard, inverse)
    )
    grads = jnp.concatenate(
        [
            outer(normed_first, grad_mixed),
            outer(grad_out, attended),
            outer(normed_second, grad_pre),
            outer(grad_out, hidden),
        ],
        axis=2,
    )
    small = jnp.concatenate(
        [
            jnp.sum(back_first * standard, axis=0),
            jnp.sum(back_first, axis=0),
            jnp.sum(back_second * standard, axis=0),
            jnp.sum(back_second, axis=0),
            jnp.sum(grad_out, axis=0, dtype=jnp.float32),
            jnp.sum(grad_mixed, axis=0, dtype=jnp.float32),
            jnp.sum(grad_pre, axis=0, dtype=jnp.float32),
        ]
    ).reshape(-1, 128)
    own_grads, small_sum = scatter_grads(grads, small, rows, cols)
    small_sum = small_sum.reshape(-1)
    gain_one, bias_one, gain_two, bias_two, out_bias = (
        small_sum[at * width : (at + 1) * width] for at in range(5)
    )
    qkv_from = 5 * width
    in_from = qkv_from + 3 * width
    qkv_bias_grad = lax.dynamic_slice_in_dim(small_sum, qkv_from + col_index * qkv_cols, qkv_cols, 0)
    fc_in_bias_grad = lax.dynamic_slice_in_dim(small_sum, in_from + col_index * ff_cols, ff_cols, 0)
    return (
        block_out,
        input_grad,
        gain_one,
        bias_one,
        gain_two,
        bias_two,
        own_grads[:, : cuts[0]],
        qkv_bias_grad,
        own_grads[:, cuts[0] : cuts[1]].T,
        out_bias,
        own_grads[:, cuts[1] : cuts[2]],
        fc_in_bias_grad,
        own_grads[:, cuts[2] :].T,
        out_bias,
    )


def solution(mesh):
    return jax.shard_map(
        on_device,
        mesh=mesh,
        in_specs=(
            P(("row", "col"), None),
            P(("row", "col"), None),
            P(("row", "col")),
            P(("row", "col")),
            P(),
            P(),
            P(),
            P(),
            P("row", "col"),
            P("col"),
            P("col", "row"),
            P(),
            P("row", "col"),
            P("col"),
            P("col", "row"),
            P(),
        ),
        out_specs=(
            P(("row", "col"), None),
            P(("row", "col"), None),
            P(),
            P(),
            P(),
            P(),
            P("row", "col"),
            P("col"),
            P("col", "row"),
            P(),
            P("row", "col"),
            P("col"),
            P("col", "row"),
            P(),
        ),
        check_vma=False,
    )
```

time: 556 us -> 301 us (0.54)
  waiting for transfers between devices: 296 us -> 0 us
  Pallas kernels: 0 us -> 152 us
  blocking collectives: 144 us -> 20.8 us
  local copies, waits for them, and re-layouts: 12.7 us -> 45.4 us
  between operations: 15.5 us -> 2.73 us
  starting transfers between devices: 7.7 us -> 0 us
    reduce_scatter x6 -> x0, waiting for transfers between devices: 164 us -> none  [the longest x1 46.3 us: on_device(): lax.psum_scatter(grad_out_w, 'row', scatter_dimension=1, tiled=True)]
    pallas_call x0 -> x2, Pallas kernels: none -> 152 us  [the longest x1 83.3 us: scatter_grads(): pl.pallas_call(scatter_kernel, out_shape=(jax.ShapeDtypeStruct(shape, jnp...]
    all_gather x5 -> x0, waiting for transfers between devices: 106 us -> none  [the longest x1 31.8 us: on_device(): grad_rows = lax.all_gather(grad_out, 'col', axis=0, tiled=True)]
    all_to_all x2 -> x0, blocking collectives: 78.4 us -> none  [the longest x1 61.8 us: on_device(): lax.all_to_all(grad_mixed, 'col', split_axis=1, concat_axis=0, tiled=True)]
    psum x1 -> x0, blocking collectives: 43.6 us -> none  [on_device(): lax.psum((norm_sums[0], norm_sums[1], norm_sums[2], norm_sums[3], jnp.sum...]
    all_to_all x2 -> x0, waiting for transfers between devices: 23.8 us -> none  [the longest x1 23.8 us: on_device(): lax.all_to_all(mixed_rows, 'col', split_axis=0, concat_axis=1, tiled=True)]
    all_gather x2 -> x0, blocking collectives: 21.8 us -> none  [the longest x1 12.3 us: on_device(): lax.all_gather(qkv_weight, 'row', axis=0, tiled=True)]
    concatenate x0 -> x3, local copies, waits for them, and re-layouts: none -> 21 us  [the longest x1 19.1 us: on_device(): jnp.concatenate([outer(normed_first, grad_mixed), outer(grad_out, attende...]
  transfers between devices with their start and end apart: 14 -> 0, of which waited for: 9 -> 0; matrix products, arithmetic and copies ran while one was open for 15% -> 0% of each run, Pallas kernels for 0% -> 0%
where the time goes in v1:
time: 301 us; the launch traced here: 299 us
  Pallas kernels  152 us (50%)
  matrix products  57.6 us (19%)
  local copies, waits for them, and re-layouts  45.4 us (15%)
  other arithmetic  21.4 us (7%)
  blocking collectives  20.8 us (7%)
    pallas_call x1, Pallas kernels, scatter_grads(): pl.pallas_call(scatter_kernel, out_shape=(jax.ShapeDtypeStruct(shape, jnp...  83.3 us
    pallas_call x1, Pallas kernels, gather_shards(): pl.pallas_call(gather_kernel, out_shape=jax.ShapeDtypeStruct((cols, rows)...  68.3 us
    unnamed x1, blocking collectives  20.8 us
    concatenate x1, local copies, waits for them, and re-layouts, on_device(): jnp.concatenate([outer(normed_first, grad_mixed), outer(grad_out, attende...  19.1 us
    dot_general x4, matrix products, narrow(): jnp.einsum('rcw,cdw->rd', split, weight, preferred_element_type=jnp.float32)  17 us
    dot_general x3, matrix products, widen(): jnp.einsum('rd,cdw->rcw', left, weight, preferred_element_type=jnp.float32)  14.5 us
    unnamed x99, local copies, waits for them, and re-layouts  8.05 us
    dot_general x4, matrix products, outer(): jnp.einsum('rd,rcw->cdw', left, split, preferred_element_type=jnp.float32)  7.1 us

profile of v1, /device:TPU:0, one launch (start us, length us, event | category | flops | bytes accessed | tf_op | source)
XLA Modules:
  0.0 299.5 jit_solution(12337881644390705422)
XLA Ops:
  0.7 1.2 slice.137
  2.5 1.2 dynamic-slice
  4.4 1.2 compare_bitcast_fusion
  6.4 1.1 convert_reduce_fusion.2
  7.6 1.2 fusion.80
  9.4 1.3 fusion.136
  10.7 1.3 fusion.110
  12.1 0.9 maximum_dynamic-update-slice_fusion
  13.0 20.8 %all-reduce = f32[5376]{0:T(1024)S(1)} all-reduce(f32[5376]{0:T(1024)S(1)} %maximum_dynamic-update-slice_fusion), channel_id=2, replica_groups=mesh['row'=8,'col'=4] {'col'}, use_global_device_ids=true, to_apply=%add | all-reduce | flops 5376 | bytes 43008
  35.9 0.9 copy.30
  36.8 0.8 fusion.91
  37.5 1.9 concatenate.79.shard
  39.4 68.3 %shard_map.263 = bf16[4,8,96,2304]{3,2,1,0:T(8,128)(2,1)} custom-call(bf16[96,2304]{1,0:T(8,128)(2,1)} %concatenate.79.shard), custom_call_target="tpu_custom_call" | custom-call | tf_op jit(solution)/shard_map/pallas_call | solution.py:209
  107.8 2.5 slice.189
  110.3 0.9 copy.48
  111.2 1.2 fusion.133
  112.6 3.9 %fusion.9 = f32[256,4,576]{0,2,1:T(8,128)S(1)} fusion(bf16[4,768,2304]{2,1,0:T(8,128)(2,1)} %bitcast.132, bf16[256,768]{1,0:T(8,128)(2,1)S(1)} %copy-done, f32[768]{0:T(1024)S(1)} %copy-done.40, f32[768]{0:T(1024)S(1)} %copy-done.26, f32[256]{0:T(256)S(1)} %copy-done.31, f32[256]{0:T(256)S(1)} %copy-done.24), kind=kOutput, calls=%fused_computation.14 | convolution fusion | flops 907149312 | bytes 6692864 | tf_op jit(solution)/shard_map/rd,cdw->rcw/dot_general | solution.py:453
  117.7 2.2 fusion.87
  121.3 1.6 convolution_convert_fusion.2
  123.0 1.6 fusion.55
  124.5 5.8 %fusion.40 = f32[256,12,64]{0,2,1:T(8,128)} fusion(f32[12,256,256]{1,2,0:T(8,128)} %fusion.87, f32[12,256,256]{1,2,0:T(8,128)S(1)} %get-tuple-element.80, f32[12,256]{1,0:T(8,128)} %copy-done.34, pred[256,256]{0,1:T(8,128)(4,1)} %fusion.91, bf16[256,12,48]{0,2,1:T(8,128)(2,1)} %copy-done.14, bf16[256,12,16]{0,2,1:T(8,128)(2,1)} %copy-done.19), kind=kOutput, calls=%fused_computation.44 | convolution fusion | flops 110103808 | bytes 7548928 | tf_op jit(solution)/shard_map/phij,pjhd->pihd/dot_general | solution.py:490
  130.4 5.9 %fusion.43 = f32[256,12,64]{0,2,1:T(8,128)} fusion(f32[12,256,256]{1,2,0:T(8,128)} %fusion.87, f32[12,256,256]{1,2,0:T(8,128)S(1)} %get-tuple-element.80, f32[12,256]{1,0:T(8,128)} %copy-done.34, pred[256,256]{0,1:T(8,128)(4,1)} %fusion.91, bf16[256,12,48]{0,2,1:T(8,128)(2,1)} %copy-done.13, bf16[256,12,16]{0,2,1:T(8,128)(2,1)} %copy-done.18), kind=kOutput, calls=%fused_computation.45 | convolution fusion | flops 110103808 | bytes 7548928 | tf_op jit(solution)/shard_map/phij,pihd->pjhd/dot_general | solution.py:493
  136.2 1.2 fusion.89
  137.4 1.1 fusion.88
  138.5 1.1 slice_multiply_fusion.3
  139.6 1.1 fusion.105
  140.8 1.2 convert_reduce_fusion.1
  142.7 3.7 %convolution_bitcast_fusion = f32[256,768]{1,0:T(8,128)} fusion(bf16[256,4,192]{0,2,1:T(8,128)(2,1)S(1)} %bitcast.146, bf16[4,768,2304]{2,1,0:T(8,128)(2,1)} %bitcast.133), kind=kOutput, calls=%fused_computation.47 | convolution fusion | flops 301989888 | bytes 2752512 | tf_op jit(solution)/shard_map/rcw,cdw->rd/dot_general | solution.py:459
  146.5 1.8 fusion.33
  148.3 2.2 convert_bitcast_fusion.2
  150.6 5.1 %multiply_convert_fusion.1 = (bf16[256,4,768]{2,0,1:T(8,128)(2,1)}, f32[256,4,768]{2,0,1:T(8,128)S(1)}) fusion(f32[4,768]{1,0:T(4,128)S(1)} %copy-done.36, bf16[4,768,2304]{2,1,0:T(8,128)(2,1)} %bitcast.134, bf16[256,768]{1,0:T(8,128)(2,1)S(1)} %copy-done.1, f32[768]{0:T(1024)S(1)} %copy-done.41, f32[768]{0:T(1024)S(1)} %copy-done.29, ...), kind=kOutput, calls=%fused_computation.28 | convolution fusion | flops 1213857792 | bytes 9850880 | tf_op jit(solution)/shard_map/rd,cdw->rcw/dot_general | solution.py:453
  155.7 5.5 %convert_reduce_fusion = (f32[4,768]{1,0:T(4,128)}, bf16[256,4,768]{2,0,1:T(8,128)(2,1)}) fusion(f32[256,4,768]{2,0,1:T(8,128)S(1)} %get-tuple-element.78, f32[4,768]{1,0:T(4,128)S(1)} %copy-done.36, bf16[4,768,2304]{2,1,0:T(8,128)(2,1)} %bitcast.135, bf16[256,768]{1,0:T(8,128)(2,1)S(1)} %copy-done.4, pred[256]{0:T(512)(128)(4,1)S(1)} %copy-done.38), kind=kOutput, calls=%fused_computation.24 | convolution fusion | flops 1218376704 | bytes 9855232 | tf_op jit(solution)/shard_map/rd,cdw->rcw/dot_general | solution.py:453
  161.9 5.6 %fusion.52 = f32[256,768]{1,0:T(8,128)} fusion(f32[256,768]{1,0:T(8,128)} %convolution_bitcast_fusion, bf16[256,4,768]{2,0,1:T(8,128)(2,1)} %get-tuple-element.77, bf16[4,768,2304]{2,1,0:T(8,128)(2,1)} %bitcast.136, bf16[256,768]{1,0:T(8,128)(2,1)} %param.16, f32[768]{0:T(1024)} %param.31, f32[768]{0:T(1024)} %param.27), kind=kOutput, calls=%fused_computation.49 | convolution fusion | flops 1208942592 | bytes 8265728 | tf_op jit(solution)/shard_map/rcw,cdw->rd/dot_general | solution.py:459
  167.5 3.9 %fusion.34 = f32[256,768]{1,0:T(8,128)S(1)} fusion(bf16[256,4,768]{2,0,1:T(8,128)(2,1)S(1)} %copy-done.10, bf16[4,768,2304]{2,1,0:T(8,128)(2,1)} %bitcast.137), kind=kOutput, calls=%fused_computation.42 | convolution fusion | flops 1207959552 | bytes 7077888 | tf_op jit(solution)/shard_map/rcw,cdw->rd/dot_general | solution.py:459
  171.5 3.8 %fusion.78 = (f32[768]{0:T(1024)S(1)}, f32[256]{0:T(256)S(1)}, f32[256]{0:T(256)S(1)}, f32[768]{0:T(1024)S(1)}, f32[768]{0:T(1024)S(1)}, /*index=5*/f32[256]{0:T...) fusion(bf16[256,768]{1,0:T(8,128)(2,1)S(1)} %copy-done.2, f32[256]{0:T(256)S(1)} %copy-done.33, ...), kind=kOutput, calls=%fused_computation.81 | convolution fusion | flops 909307904 | bytes 7102464 | tf_op jit(solution)/shard_map/rcw,cdw->rd/dot_general | solution.py:459
  175.4 1.4 convert_reduce_fusion.3
  177.5 1.6 convert_bitcast_fusion.1
  179.1 1.5 convert_bitcast_fusion
  180.6 6.5 %pad_maximum_fusion = bf16[4,768,2304]{1,2,0:T(8,128)(2,1)} fusion(bf16[4,768,768]{1,2,0:T(8,128)(2,1)S(1)} %convert_bitcast_fusion, bf16[4,768,768]{1,2,0:T(8,128)(2,1)S(1)} %convert_bitcast_fusion.1, bf16[4,768,192]{1,2,0:T(8,128)(2,1)S(1)} %copy-done.6, bf16[4,768,576]{1,2,0:T(8,128)(2,1)S(1)} %convert_bitcast_fusion.2), kind=kLoop, calls=%fused_computation.1 | loop fusion | flops 56623104 | bytes 28311552 | tf_op jit(solution)/shard_map/concatenate | solution.py:514
  187.1 19.1 %copy.39 = bf16[4,768,2304]{2,1,0:T(8,128)(2,1)} copy(bf16[4,768,2304]{1,2,0:T(8,128)(2,1)} %pad_maximum_fusion) | data formatting | bytes 28311552 | tf_op jit(solution)/shard_map/concatenate | solution.py:514
  206.2 83.3 %shard_map.264 = (f32[96,2304]{1,0:T(8,128)}, f32[72,128]{1,0:T(8,128)}) custom-call(bf16[4,8,96,2304]{3,2,1,0:T(8,128)(2,1)} %bitcast.130, f32[72,128]{1,0:T(8,128)} %bitcast.150), custom_call_target="tpu_custom_call" | custom-call | tf_op jit(solution)/shard_map/pallas_call | solution.py:367
  289.5 1.4 dynamic_slice.7
  290.8 1.4 dynamic_slice.6
  292.2 1.4 slice_bitcast_fusion.7
  293.6 1.0 slice_bitcast_fusion.6
  294.6 0.7 copy.40
  295.3 1.7 slice.170
  297.0 1.9 slice_bitcast_fusion.5
  (125 shorter events, 8.9 us)
Async XLA Ops:
  7.6 4.5 %copy-start.23 = (f32[256]{0:T(256)}, f32[256]{0:T(256)S(1)}, u32[]{:S(2)}) copy-start(f32[256]{0:T(256)S(1)} %broadcast_multiply_fusion.5) | copy-start | bytes 3076
  107.8 3.4 %copy-start.3 = (bf16[256,768]{1,0:T(8,128)(2,1)S(1)}, bf16[256,768]{1,0:T(8,128)(2,1)}, u32[]{:S(2)}) copy-start(bf16[256,768]{1,0:T(8,128)(2,1)} %param.17) | copy-start | bytes 1179652
  110.3 2.2 copy-start
  111.1 1.4 copy-start.24
  111.1 1.4 copy-start.26
  111.2 1.4 copy-start.31
  111.2 1.4 copy-start.40
  112.5 3.9 %copy-start.17 = (f32[3,12,64]{2,1,0:T(8,128)S(1)}, f32[3,12,64]{2,1,0:T(8,128)}, u32[]{:S(2)}) copy-start(f32[3,12,64]{2,1,0:T(8,128)} %add.173) | copy-start | bytes 27652
  116.9 0.7 copy-start.16
  117.1 2.8 copy-start.14
  117.1 2.8 copy-start.15
  117.2 3.4 %copy-start.13 = (bf16[256,12,48]{0,2,1:T(8,128)(2,1)}, bf16[256,12,48]{0,2,1:T(8,128)(2,1)S(1)}, u32[]{:S(2)}) copy-start(bf16[256,12,48]{0,2,1:T(8,128)(2,1)S(1)} %slice.183) | copy-start | bytes 884740
  117.7 3.0 copy-start.18
  117.7 3.0 copy-start.19
  121.3 1.6 copy-start.34
  136.2 4.5 %copy-start.11 = (bf16[256,1,12,64]{0,3,2,1:T(8,128)(2,1)S(1)}, bf16[256,1,12,64]{0,3,2,1:T(8,128)(2,1)}, u32[]{:S(2)}) copy-start(bf16[256,1,12,64]{0,3,2,1:T(8,128)(2,1)} %fusion.55) | copy-start | bytes 1179652
  136.2 6.5 %copy-start.12 = (bf16[12,64,256]{2,1,0:T(8,128)(2,1)S(1)}, bf16[12,64,256]{2,1,0:T(8,128)(2,1)}, u32[]{:S(2)}) copy-start(bf16[12,64,256]{2,1,0:T(8,128)(2,1)} %convolution_convert_fusion.2) | copy-start | bytes 1179652
  139.6 6.8 %copy-start.37 = (pred[256]{0:T(512)(128)(4,1)S(1)}, pred[256]{0:T(512)(128)(4,1)}, u32[]{:S(2)}) copy-start(pred[256]{0:T(512)(128)(4,1)} %compare_bitcast_fusion) | copy-start | bytes 772
  140.7 7.6 %copy-start.25 = (f32[256]{0:T(256)S(1)}, f32[256]{0:T(256)}, u32[]{:S(2)}) copy-start(f32[256]{0:T(256)} %copy-done.23) | copy-start | bytes 3076
  140.8 7.5 %copy-start.27 = (f32[768]{0:T(1024)S(1)}, f32[768]{0:T(1024)}, u32[]{:S(2)}) copy-start(f32[768]{0:T(1024)} %param.20) | copy-start | bytes 9220
  140.8 7.5 %copy-start.32 = (f32[256]{0:T(256)S(1)}, f32[256]{0:T(256)}, u32[]{:S(2)}) copy-start(f32[256]{0:T(256)} %add_rsqrt_fusion) | copy-start | bytes 3076
  142.7 5.6 %copy-start.7 = (bf16[256,3,12,64]{0,3,2,1:T(8,128)(2,1)S(1)}, bf16[256,3,12,64]{0,3,2,1:T(8,128)(2,1)}, u32[]{:S(2)}) copy-start(bf16[256,3,12,64]{0,3,2,1:T(8,128)(2,1)} %get-tuple-element.45) | copy-start | bytes 3538948
  146.5 4.1 %copy-start.1 = (bf16[256,768]{1,0:T(8,128)(2,1)S(1)}, bf16[256,768]{1,0:T(8,128)(2,1)}, u32[]{:S(2)}) copy-start(bf16[256,768]{1,0:T(8,128)(2,1)} %param.16) | copy-start | bytes 1179652
  146.5 4.1 %copy-start.29 = (f32[768]{0:T(1024)S(1)}, f32[768]{0:T(1024)}, u32[]{:S(2)}) copy-start(f32[768]{0:T(1024)} %param.22) | copy-start | bytes 9220
  146.5 4.1 %copy-start.36 = (f32[4,768]{1,0:T(4,128)S(1)}, f32[4,768]{1,0:T(4,128)}, u32[]{:S(2)}) copy-start(f32[4,768]{1,0:T(4,128)} %slice.191) | copy-start | bytes 36868
  146.5 4.1 %copy-start.41 = (f32[768]{0:T(1024)S(1)}, f32[768]{0:T(1024)}, u32[]{:S(2)}) copy-start(f32[768]{0:T(1024)} %param.23) | copy-start | bytes 9220
  150.6 5.1 %copy-start.4 = (bf16[256,768]{1,0:T(8,128)(2,1)S(1)}, bf16[256,768]{1,0:T(8,128)(2,1)}, u32[]{:S(2)}) copy-start(bf16[256,768]{1,0:T(8,128)(2,1)} %param.17) | copy-start | bytes 1179652
  150.6 5.1 %copy-start.38 = (pred[256]{0:T(512)(128)(4,1)S(1)}, pred[256]{0:T(512)(128)(4,1)}, u32[]{:S(2)}) copy-start(pred[256]{0:T(512)(128)(4,1)} %compare_bitcast_fusion) | copy-start | bytes 772
  161.9 5.6 %copy-start.10 = (bf16[256,4,768]{2,0,1:T(8,128)(2,1)S(1)}, bf16[256,4,768]{2,0,1:T(8,128)(2,1)}, u32[]{:S(2)}) copy-start(bf16[256,4,768]{2,0,1:T(8,128)(2,1)} %get-tuple-element.83) | copy-start | bytes 4718596
  167.5 3.9 %copy-start.2 = (bf16[256,768]{1,0:T(8,128)(2,1)S(1)}, bf16[256,768]{1,0:T(8,128)(2,1)}, u32[]{:S(2)}) copy-start(bf16[256,768]{1,0:T(8,128)(2,1)} %param.16) | copy-start | bytes 1179652
  167.5 3.9 %copy-start.8 = (bf16[256,3,12,64]{0,3,2,1:T(8,128)(2,1)S(1)}, bf16[256,3,12,64]{0,3,2,1:T(8,128)(2,1)}, u32[]{:S(2)}) copy-start(bf16[256,3,12,64]{0,3,2,1:T(8,128)(2,1)} %get-tuple-element.45) | copy-start | bytes 3538948
  167.5 3.9 %copy-start.28 = (f32[768]{0:T(1024)S(1)}, f32[768]{0:T(1024)}, u32[]{:S(2)}) copy-start(f32[768]{0:T(1024)} %param.20) | copy-start | bytes 9220
  167.5 3.9 %copy-start.30 = (f32[768]{0:T(1024)S(1)}, f32[768]{0:T(1024)}, u32[]{:S(2)}) copy-start(f32[768]{0:T(1024)} %param.22) | copy-start | bytes 9220
  167.5 3.9 %copy-start.33 = (f32[256]{0:T(256)S(1)}, f32[256]{0:T(256)}, u32[]{:S(2)}) copy-start(f32[256]{0:T(256)} %add_rsqrt_fusion) | copy-start | bytes 3076
  171.4 3.9 %copy-start.21 = (f32[9216]{0:T(1024)S(1)}, f32[9216]{0:T(1024)}, u32[]{:S(2)}) copy-start(f32[9216]{0:T(1024)} %custom-call) | copy-start | bytes 110596
  171.4 4.0 %copy-start.5 = (bf16[256,768]{1,0:T(8,128)(2,1)S(1)}, bf16[256,768]{1,0:T(8,128)(2,1)}, u32[]{:S(2)}) copy-start(bf16[256,768]{1,0:T(8,128)(2,1)} %param.17) | copy-start | bytes 1179652
  171.5 4.0 %copy-start.39 = (pred[256]{0:T(512)(128)(4,1)S(1)}, pred[256]{0:T(512)(128)(4,1)}, u32[]{:S(2)}) copy-start(pred[256]{0:T(512)(128)(4,1)} %compare_bitcast_fusion) | copy-start | bytes 772
  175.3 1.6 copy-start.20
  175.3 2.2 copy-start.42
  176.9 0.6 copy-start.22
  177.5 1.6 copy-start.9
  179.1 1.5 copy-start.6
  293.6 5.9 %copy-start.35 = (f32[768]{0:T(1024)}, f32[768]{0:T(1024)S(1)}, u32[]{:S(2)}) copy-start(f32[768]{0:T(1024)S(1)} %get-tuple-element.113) | copy-start | bytes 9220

commit v2 on v1

--- a/solution.py
+++ b/solution.py
@@ -139,10 +139,10 @@
             copy.wait_send()
 
 
-GATHER_COPIES = 39
-
-
-def gather_kernel(shard, out, own_sem, send_sems, recv_sems):
+GATHER_COPIES = 42
+
+
+def gather_kernel(shard, bias, out, bias_out, own_sem, send_sems, recv_sems):
     row, col, beside, across, above = partners()
     diagonal = across + 4 - 8 * (across // 4)
     half = shard.shape[0] // 2
@@ -151,6 +151,7 @@
     sends = Sends(send_sems, recv_sems)
     own = pltpu.make_async_copy(shard, out.at[col, row], own_sem)
     own.start()
+    bias_out[col] = bias[...]
 
     def share(step):
         at = (col - step + RING_COLS) % RING_COLS
@@ -161,6 +162,7 @@
             for hop in (1, 2, 3):
                 there = (col + hop) % RING_COLS
                 sends.start(("z", hop), shard, out.at[col, row], (row, there))
+                sends.start(("b", hop), bias, bias_out.at[col], (row, there))
         sends.start(("c", step), piece, out.at[at, row], (beside, col))
 
     def relay(step):
@@ -197,31 +199,36 @@
     for step in range(RING_COLS):
         for kind in ("c", "cx", "cy", "cdx", "cdy"):
             sends.arrived((kind, step))
+    for hop in (1, 2, 3):
+        sends.arrived(("b", hop))
     sends.finish()
     own.wait()
 
 
-def gather_shards(shard, rows, cols):
+def gather_shards(shard, bias, rows, cols):
     if (rows, cols) != (RING_ROWS, RING_COLS):
         return lax.all_gather(shard, ("col", "row"), axis=0, tiled=True).reshape(
             cols, rows * shard.shape[0], shard.shape[1]
-        )
-    gathered = pl.pallas_call(
+        ), lax.all_gather(bias, "col", axis=0, tiled=False)
+    gathered, biases = pl.pallas_call(
         gather_kernel,
-        out_shape=jax.ShapeDtypeStruct((cols, rows) + shard.shape, shard.dtype),
-        in_specs=[pl.BlockSpec(memory_space=pl.ANY)],
-        out_specs=pl.BlockSpec(memory_space=pl.ANY),
+        out_shape=(
+            jax.ShapeDtypeStruct((cols, rows) + shard.shape, shard.dtype),
+            jax.ShapeDtypeStruct((cols,) + bias.shape, bias.dtype),
+        ),
+        in_specs=[pl.BlockSpec(memory_space=pl.ANY), pl.BlockSpec(memory_space=pltpu.VMEM)],
+        out_specs=(pl.BlockSpec(memory_space=pl.ANY), pl.BlockSpec(memory_space=pltpu.VMEM)),
         scratch_shapes=[
             pltpu.SemaphoreType.DMA,
             pltpu.SemaphoreType.DMA((GATHER_COPIES,)),
             pltpu.SemaphoreType.DMA((GATHER_COPIES,)),
         ],
         compiler_params=pltpu.CompilerParams(collective_id=0, has_side_effects=True),
-    )(shard)
-    return gathered.reshape(cols, rows * shard.shape[0], shard.shape[1])
-
-
-SCATTER_COPIES = 40
+    )(shard, bias)
+    return gathered.reshape(cols, rows * shard.shape[0], shard.shape[1]), biases
+
+
+SCATTER_COPIES = 80
 
 
 def add_rows(target, source, start, count):
@@ -237,9 +244,13 @@
 
 
 def scatter_kernel(
-    grads,
+    grads_att,
+    grads_in,
+    grads_out,
     small,
-    out,
+    out_att,
+    out_in,
+    out_out,
     small_out,
     total,
     from_core,
@@ -257,7 +268,9 @@
     row, col, beside, across, above = partners()
     diagonal = across + 4 - 8 * (across // 4)
     chips = (row, across, above, diagonal)
-    height = out.shape[0]
+    height, part = out_att.shape
+    outs = (out_att, out_in, out_out)
+    lanes = [pl.ds(at * part, part) for at in range(len(outs))]
     half = height // 2
     low, high = pl.ds(0, half), pl.ds(half, half)
     order = (1, 2, 3, 0)
@@ -287,20 +300,30 @@
         for place in places:
             chip = chips[place]
             other = chip + 1 - 2 * (chip % 2)
-            sends.start(
-                ("c", step, place), grads.at[at, other], from_core.at[step, place], (beside, col)
-            )
-            load = pltpu.make_async_copy(
-                grads.at[at, chip], total.at[step, place], own_sems.at[step * 4 + place]
-            )
-            load.start()
-            loads[step, place] = load
+            columns = pl.ds(pl.multiple_of(at * part, 128), part)
+            away = pl.ds(pl.multiple_of(other * height, 16), height)
+            kept = pl.ds(pl.multiple_of(chip * height, 16), height)
+            for index, grads in enumerate((grads_att, grads_in, grads_out)):
+                sends.start(
+                    ("c", step, place, index),
+                    grads.at[away, columns],
+                    from_core.at[step, place, :, lanes[index]],
+                    (beside, col),
+                )
+                load = pltpu.make_async_copy(
+                    grads.at[kept, columns],
+                    total.at[step, place, :, lanes[index]],
+                    own_sems.at[(step * 4 + place) * 3 + index],
+                )
+                load.start()
+                loads[step, place, index] = load
     send_small(0)
 
     def pair(step):
         for place in places:
-            loads[step, place].wait()
-            sends.arrived(("c", step, place))
+            for index in range(len(outs)):
+                loads[step, place, index].wait()
+                sends.arrived(("c", step, place, index))
             add_rows(total.at[step, place], from_core.at[step, place], 0, height)
             if place == DIAGONAL:
                 sends.start(
@@ -342,39 +365,46 @@
     @pl.loop(0, height // 16)
     def _(tile):
         rows = pl.ds(pl.multiple_of(tile * 16, 16), 16)
-        out[rows, :] = (
-            total[0, SELF, rows, :].astype(jnp.float32)
-            + from_z[0, rows, :].astype(jnp.float32)
-            + from_z[1, rows, :].astype(jnp.float32)
-            + from_z[2, rows, :].astype(jnp.float32)
-        )
+        for index, out in enumerate(outs):
+            out[rows, :] = (
+                total[0, SELF, rows, lanes[index]].astype(jnp.float32)
+                + from_z[0, rows, lanes[index]].astype(jnp.float32)
+                + from_z[1, rows, lanes[index]].astype(jnp.float32)
+                + from_z[2, rows, lanes[index]].astype(jnp.float32)
+            )
 
     sends.finish()
 
 
 def scatter_grads(grads, small, rows, cols):
-    height, width = grads.shape[1] // rows, grads.shape[2]
+    height, width = grads[0].shape[0] // rows, grads[0].shape[1] // cols
     if (rows, cols) != (RING_ROWS, RING_COLS):
-        flat = grads.reshape(cols * rows * height, width)
-        return (
-            lax.psum_scatter(flat, ("col", "row"), scatter_dimension=0, tiled=True).astype(
-                jnp.float32
-            ),
-            lax.psum(small, ("row", "col")),
-        )
-    kind = grads.dtype
-    shape = (height, width)
+        own = [
+            lax.psum_scatter(
+                lax.psum_scatter(
+                    grad.reshape(rows * height, cols, width).swapaxes(0, 1),
+                    "col",
+                    scatter_dimension=0,
+                    tiled=False,
+                ),
+                "row",
+                scatter_dimension=0,
+                tiled=True,
+            ).astype(jnp.float32)
+            for grad in grads
+        ]
+        return (*own, lax.psum(small, ("row", "col")))
+    kind = grads[0].dtype
+    shape = (height, len(grads) * width)
     return pl.pallas_call(
         scatter_kernel,
         out_shape=(
-            jax.ShapeDtypeStruct(shape, jnp.float32),
+            *[jax.ShapeDtypeStruct((height, width), jnp.float32)] * len(grads),
             jax.ShapeDtypeStruct(small.shape, small.dtype),
         ),
-        in_specs=[pl.BlockSpec(memory_space=pl.ANY), pl.BlockSpec(memory_space=pltpu.VMEM)],
-        out_specs=(
-            pl.BlockSpec(memory_space=pltpu.VMEM),
-            pl.BlockSpec(memory_space=pltpu.VMEM),
-        ),
+        in_specs=[pl.BlockSpec(memory_space=pl.ANY)] * len(grads)
+        + [pl.BlockSpec(memory_space=pltpu.VMEM)],
+        out_specs=(pl.BlockSpec(memory_space=pltpu.VMEM),) * (len(grads) + 1),
         scratch_shapes=[
             pltpu.VMEM((cols, 4) + shape, kind),
             pltpu.VMEM((cols, 4) + shape, kind),
@@ -385,14 +415,14 @@
             pltpu.VMEM((cols - 1,) + shape, kind),
             pltpu.VMEM((5,) + small.shape, small.dtype),
             pltpu.VMEM((5,) + small.shape, small.dtype),
-            pltpu.SemaphoreType.DMA((16,)),
+            pltpu.SemaphoreType.DMA((16 * len(grads),)),
             pltpu.SemaphoreType.DMA((SCATTER_COPIES,)),
             pltpu.SemaphoreType.DMA((SCATTER_COPIES,)),
         ],
         compiler_params=pltpu.CompilerParams(
             collective_id=1, has_side_effects=True, vmem_limit_bytes=56 * 2**20
         ),
-    )(grads.reshape(cols, rows, height, width), small)
+    )(*grads, small)
 
 
 def on_device(
@@ -430,10 +460,10 @@
     cuts = (qkv_cols, qkv_cols + att_cols, qkv_cols + att_cols + ff_cols)
 
     shard = jnp.concatenate([qkv_weight, dense_weight.T, fc_in_weight, fc_out_weight.T], axis=1)
-    biases = lax.all_gather(jnp.concatenate([qkv_bias, fc_in_bias]), "col", axis=0, tiled=False)
-    qkv_bias_full = biases[:, :qkv_cols].reshape(-1)
-    fc_in_bias_full = biases[:, qkv_cols:].reshape(-1)
-    gathered = gather_shards(shard, rows, cols)
+    bias = jnp.concatenate([qkv_bias, fc_in_bias])[None, :]
+    gathered, biases = gather_shards(shard, bias, rows, cols)
+    qkv_bias_full = biases[:, 0, :qkv_cols].reshape(-1)
+    fc_in_bias_full = biases[:, 0, qkv_cols:].reshape(-1)
     qkv_full = gathered[:, :, : cuts[0]]
     dense_full = gathered[:, :, cuts[0] : cuts[1]]
     fc_in_full = gathered[:, :, cuts[1] : cuts[2]]
@@ -459,9 +489,8 @@
         return jnp.einsum("rcw,cdw->rd", split, weight, preferred_element_type=jnp.float32)
 
     def outer(left, right):
-        split = right.reshape(right.shape[0], cols, -1)
-        return jnp.einsum(
-            "rd,rcw->cdw", left, split, preferred_element_type=jnp.float32
+        return lax.dot_general(
+            left, right, (((0,), (0,)), ((), ())), preferred_element_type=jnp.float32
         ).astype(jnp.bfloat16)
 
     mixed = (widen(normed_first, qkv_full) + qkv_bias_full).astype(jnp.bfloat16)
@@ -511,14 +540,19 @@
         + norm_back(back_first, norm1_gain, standard, inverse)
         + norm_back(back_second, norm2_gain, standard, inverse)
     )
-    grads = jnp.concatenate(
-        [
-            outer(normed_first, grad_mixed),
-            outer(grad_out, attended),
-            outer(normed_second, grad_pre),
-            outer(grad_out, hidden),
-        ],
-        axis=2,
+    mixed_cols = jnp.pad(
+        grad_mixed.reshape(own_rows, cols, qkv_cols), ((0, 0), (0, 0), (0, att_cols))
+    ).reshape(own_rows, -1)
+    attended_cols = jnp.pad(
+        attended.reshape(own_rows, cols, att_cols), ((0, 0), (0, 0), (qkv_cols, 0))
+    ).reshape(own_rows, -1)
+    grads = (
+        outer(
+            jnp.concatenate([normed_first, grad_out], axis=0),
+            jnp.concatenate([mixed_cols, attended_cols], axis=0),
+        ),
+        outer(normed_second, grad_pre),
+        outer(grad_out, hidden),
     )
     small = jnp.concatenate(
         [
@@ -531,7 +565,7 @@
             jnp.sum(grad_pre, axis=0, dtype=jnp.float32),
         ]
     ).reshape(-1, 128)
-    own_grads, small_sum = scatter_grads(grads, small, rows, cols)
+    att_grads, in_grads, out_grads, small_sum = scatter_grads(grads, small, rows, cols)
     small_sum = small_sum.reshape(-1)
     gain_one, bias_one, gain_two, bias_two, out_bias = (
         small_sum[at * width : (at + 1) * width] for at in range(5)
@@ -547,13 +581,13 @@
         bias_one,
         gain_two,
         bias_two,
-        own_grads[:, : cuts[0]],
+        att_grads[:, :qkv_cols],
         qkv_bias_grad,
-        own_grads[:, cuts[0] : cuts[1]].T,
+        att_grads[:, qkv_cols:].T,
         out_bias,
-        own_grads[:, cuts[1] : cuts[2]],
+        in_grads,
         fc_in_bias_grad,
-        own_grads[:, cuts[2] :].T,
+        out_grads.T,
         out_bias,
     )
 

time: 301 us -> 296 us (0.983)
  blocking collectives: 20.8 us -> 0 us
  Pallas kernels: 152 us -> 164 us
  matrix products: 57.6 us -> 69.1 us
  local copies, waits for them, and re-layouts: 45.4 us -> 37.3 us
    unnamed x1 -> x0, blocking collectives: 20.8 us -> none
    concatenate x1 -> x0, local copies, waits for them, and re-layouts: 19.1 us -> none  [on_device(): jnp.concatenate([outer(normed_first, grad_mixed), outer(grad_out, attende...]
    pallas_call x2, Pallas kernels: 152 us -> 164 us  [the longest x1 90.3 us: scatter_grads(): pl.pallas_call(scatter_kernel, out_shape=(*[jax.ShapeDtypeStruct((height,...]
    dot_general x0 -> x2, local copies, waits for them, and re-layouts: none -> 6.1 us  [widen(): jnp.einsum('rd,cdw->rcw', left, weight, preferred_element_type=jnp.float32)]
    concatenate x1, other arithmetic: 6.51 us -> 0.78 us  [on_device(): bias = jnp.concatenate([qkv_bias, fc_in_bias])[None, :]]
    convert_element_type x0 -> x2, other arithmetic: none -> 5.01 us  [the longest x1 3.75 us: on_device(): hidden = gelu_exact(pre_act).astype(jnp.bfloat16)]
    dot_general x4 -> x3, matrix products: 7.1 us -> 11.9 us  [outer(): lax.dot_general(left, right, (((0,), (0,)), ((), ())), preferred_element_...]
    unnamed x99 -> x98, local copies, waits for them, and re-layouts: 8.05 us -> 11 us
where the time goes in v2:
time: 296 us; the launch traced here: 294 us
  Pallas kernels  164 us (55%)
  matrix products  69.1 us (23%)
  local copies, waits for them, and re-layouts  37.3 us (13%)
  other arithmetic  21.7 us (7%)
    pallas_call x1, Pallas kernels, scatter_grads(): pl.pallas_call(scatter_kernel, out_shape=(*[jax.ShapeDtypeStruct((height,...  90.3 us
    pallas_call x1, Pallas kernels, gather_shards(): pl.pallas_call(gather_kernel, out_shape=(jax.ShapeDtypeStruct((cols, rows...  73.9 us
    dot_general x4, matrix products, narrow(): jnp.einsum('rcw,cdw->rd', split, weight, preferred_element_type=jnp.float32)  17 us
    dot_general x3, matrix products, widen(): jnp.einsum('rd,cdw->rcw', left, weight, preferred_element_type=jnp.float32)  15.6 us
    dot_general x3, matrix products, outer(): lax.dot_general(left, right, (((0,), (0,)), ((), ())), preferred_element_...  11.9 us
    unnamed x98, local copies, waits for them, and re-layouts  11 us
    dot_general x1, matrix products, on_device(): jnp.einsum('phij,pihd->pjhd', grad_scores, queries, preferred_element_typ...  7.7 us
    dot_general x1, matrix products, on_device(): jnp.einsum('phij,pjhd->pihd', grad_scores, key_rows, preferred_element_ty...  7.67 us

profile of v2, /device:TPU:0, one launch (start us, length us, event | category | flops | bytes accessed | tf_op | source)
XLA Modules:
  0.0 294.4 jit_solution(8343917997037113073)
XLA Ops:
  0.7 1.2 slice.131
  4.0 1.1 convert_reduce_fusion.2
  5.2 1.2 fusion.88
  6.4 1.3 fusion.145
  7.7 1.3 fusion.115
  9.1 0.8 pad_maximum_fusion.8
  11.1 0.9 copy.38
  12.0 0.8 fusion.100
  12.8 1.3 fusion.76
  14.1 2.0 concatenate.82.shard
  16.1 1.8 convert_reduce_fusion.3
  17.9 73.9 %shard_map.263 = (bf16[4,8,96,2304]{3,2,1,0:T(8,128)(2,1)}, f32[4,1,1344]{2,1,0:T(1,128)}) custom-call(bf16[96,2304]{1,0:T(8,128)(2,1)} %concatenate.82.shard, f32[1,1344]{1,0:T(1,128)} %broadcast_in_dim.37.bias), custom_call_target="tpu_custom_call" | custom-call | tf_op jit(solution)/shard_map/pallas_call | solution.py:213
  92.6 0.8 slice.146
  94.7 2.4 slice.180
  98.4 3.9 %fusion.9 = f32[256,4,576]{0,2,1:T(8,128)S(1)} fusion(bf16[4,768,2304]{2,1,0:T(8,128)(2,1)} %bitcast.144, bf16[256,768]{1,0:T(8,128)(2,1)S(1)} %fusion.76), kind=kOutput, calls=%fused_computation.14 | convolution fusion | flops 905969664 | bytes 6684672 | tf_op jit(solution)/shard_map/rd,cdw->rcw/dot_general | solution.py:483
  105.3 5.5 %fusion.7 = f32[256,4,768]{2,0,1:T(8,128)} fusion(bf16[4,768,2304]{2,1,0:T(8,128)(2,1)} %bitcast.145, bf16[256,768]{1,0:T(8,128)(2,1)S(1)} %copy-done, f32[768]{0:T(1024)S(1)} %copy-done.23, f32[768]{0:T(1024)S(1)} %copy-done.20, f32[256]{0:T(256)S(1)} %copy-done.33, f32[256]{0:T(256)S(1)} %copy-done.27), kind=kOutput, calls=%fused_computation.12 | convolution fusion | flops 1209139200 | bytes 8265728 | tf_op jit(solution)/shard_map/rd,cdw->rcw/dot_general | solution.py:483
  110.8 2.2 fusion.96
  113.0 2.6 copy.46
  115.6 1.8 fusion.31
  118.2 3.1 %convolution_convert_fusion.4 = bf16[12,64,256]{2,1,0:T(8,128)(2,1)} fusion(bf16[256,3,12,64]{0,3,2,1:T(8,128)(2,1)} %copy-done.7, f32[12,256]{1,0:T(8,128)S(1)} %log_add_fusion, f32[12,256,256]{1,2,0:T(8,128)S(1)} %get-tuple-element.102, pred[256,256]{0,1:T(8,128)(4,1)S(1)} %copy-done.16), kind=kOutput, calls=%fused_computation.63 | convolution fusion | flops 104005632 | bytes 4009984 | tf_op jit(solution)/shard_map/phij,pjhd->pihd/dot_general | solution.py:508
  121.3 1.6 fusion.63
  122.9 7.7 %fusion.45 = f32[256,12,64]{0,2,1:T(8,128)} fusion(f32[12,256,256]{1,2,0:T(8,128)} %fusion.96, f32[12,256,256]{1,2,0:T(8,128)} %copy-done.9, f32[12,256]{1,0:T(8,128)} %copy-done.38, pred[256,256]{0,1:T(8,128)(4,1)} %fusion.100, bf16[256,12,48]{0,2,1:T(8,128)(2,1)} %slice.179, bf16[256,12,16]{0,2,1:T(8,128)(2,1)} %get-tuple-element.92), kind=kOutput, calls=%fused_computation.55 | convolution fusion | flops 110103808 | bytes 7548928 | tf_op jit(solution)/shard_map/phij,pjhd->pihd/dot_general | solution.py:519
  130.6 7.7 %fusion.48 = f32[256,12,64]{0,2,1:T(8,128)} fusion(f32[12,256,256]{1,2,0:T(8,128)} %fusion.96, f32[12,256,256]{1,2,0:T(8,128)} %copy-done.9, f32[12,256]{1,0:T(8,128)} %copy-done.38, pred[256,256]{0,1:T(8,128)(4,1)} %fusion.100, bf16[256,12,48]{0,2,1:T(8,128)(2,1)} %slice.174, bf16[256,12,16]{0,2,1:T(8,128)(2,1)} %get-tuple-element.91), kind=kOutput, calls=%fused_computation.56 | convolution fusion | flops 110103808 | bytes 7548928 | tf_op jit(solution)/shard_map/phij,pihd->pjhd/dot_general | solution.py:522
  138.3 1.1 fusion.98
  139.4 1.1 fusion.97
  140.5 1.1 slice_multiply_fusion.3
  141.7 1.1 fusion.110
  142.8 1.9 convert_reduce_fusion.1
  144.7 1.4 reduce_sum.153
  146.1 2.9 convolution_bitcast_fusion
  149.0 6.0 %fusion.60 = f32[256,768]{1,0:T(8,128)} fusion(f32[256,768]{1,0:T(8,128)S(1)} %convolution_bitcast_fusion, bf16[4,768,2304]{2,1,0:T(8,128)(2,1)} %bitcast.147, f32[256,4,768]{2,0,1:T(8,128)} %fusion.7, f32[4,768]{1,0:T(4,128)S(1)} %bitcast.156, bf16[256,768]{1,0:T(8,128)(2,1)S(1)} %copy-done, f32[768]{0:T(1024)S(1)} %copy-done.41, f32[768]{0:T(1024)} %param.27), kind=kOutput, calls=%fused_computation.61 | convolution fusion | flops 1213661184 | bytes 9849856 | tf_op jit(solution)/shard_map/rcw,cdw->rd/dot_general | solution.py:489
  156.2 4.5 %convolution_convert_fusion.2.grads_att = bf16[768,3072]{1,0:T(8,128)(2,1)} fusion(bf16[256,3072]{0,1:T(8,128)(2,1)S(1)} %bitcast.136, bf16[256,3072]{0,1:T(8,128)(2,1)S(1)} %bitcast.135, bf16[256,768]{1,0:T(8,128)(2,1)S(1)} %copy-done.2, bf16[256,768]{1,0:T(8,128)(2,1)S(1)} %copy-done.14), kind=kOutput, calls=%fused_computation.3 | convolution fusion | flops 2426142720 | bytes 8650752 | tf_op jit(solution)/shard_map/dot_general | solution.py:492
  160.6 6.2 %convert_reduce_fusion = (f32[4,768]{1,0:T(4,128)}, bf16[256,4,768]{2,0,1:T(8,128)(2,1)}, f32[256,4,768]{2,0,1:T(8,128)}) fusion(f32[256,4,768]{2,0,1:T(8,128)S(1)} %copy-done.8, f32[4,768]{1,0:T(4,128)S(1)} %bitcast.157, bf16[4,768,2304]{2,1,0:T(8,128)(2,1)} %bitcast.148, bf16[256,768]{1,0:T(8,128)(2,1)S(1)} %copy-done.2), kind=kOutput, calls=%fused_computation.34 | convolution fusion | flops 1218180096 | bytes 13000704 | tf_op jit(solution)/shard_map/rd,cdw->rcw/dot_general | solution.py:483
  167.6 4.3 %fusion.42 = f32[256,768]{1,0:T(8,128)S(1)} fusion(bf16[256,4,768]{2,0,1:T(8,128)(2,1)} %get-tuple-element.67, bf16[4,768,2304]{2,1,0:T(8,128)(2,1)} %bitcast.149), kind=kOutput, calls=%fused_computation.54 | convolution fusion | flops 1207959552 | bytes 7077888 | tf_op jit(solution)/shard_map/rcw,cdw->rd/dot_general | solution.py:489
  172.0 3.8 %fusion.86 = (f32[768]{0:T(1024)S(1)}, f32[256]{0:T(256)S(1)}, f32[256]{0:T(256)S(1)}, f32[768]{0:T(1024)S(1)}, f32[768]{0:T(1024)S(1)}, /*index=5*/f32[256]{0:T...) fusion(bf16[256,768]{1,0:T(8,128)(2,1)S(1)} %copy-done, f32[256]{0:T(256)S(1)} %copy-done.34, ...), kind=kOutput, calls=%fused_computation.93 | convolution fusion | flops 909307904 | bytes 7102464 | tf_op jit(solution)/shard_map/rcw,cdw->rd/dot_general | solution.py:489
  176.5 1.4 fusion.85
  177.9 3.5 %copy.45 = f32[256,4,768]{0,2,1:T(8,128)} copy(f32[256,4,768]{2,0,1:T(8,128)} %get-tuple-element.103) | data formatting | bytes 6291456 | tf_op jit(solution)/shard_map/rd,cdw->rcw/dot_general | solution.py:483
  181.4 3.7 %multiply_convert_fusion = (bf16[256,3072]{0,1:T(8,128)(2,1)S(1)}, bf16[256,3072]{0,1:T(8,128)(2,1)S(1)}) fusion(f32[256,4,768]{0,2,1:T(8,128)S(1)} %copy.46, f32[3072]{0:T(1024)S(1)} %bitcast.152, f32[256,4,768]{0,2,1:T(8,128)} %copy.45), kind=kLoop, calls=%fused_computation.35 | loop fusion | flops 11010048 | bytes 9449472 | tf_op jit(solution)/shard_map/convert_element_type | solution.py:511
  185.2 3.6 %convolution_convert_fusion.grads_out = bf16[768,3072]{1,0:T(8,128)(2,1)} fusion(bf16[256,768]{1,0:T(8,128)(2,1)S(1)} %copy-done.4, bf16[256,3072]{0,1:T(8,128)(2,1)S(1)} %get-tuple-element.72), kind=kOutput, calls=%fused_computation.1 | convolution fusion | flops 1210318848 | bytes 6684672 | tf_op jit(solution)/shard_map/dot_general | solution.py:492
  188.9 3.8 %convolution_convert_fusion.1.grads_in = bf16[768,3072]{1,0:T(8,128)(2,1)} fusion(bf16[256,3072]{0,1:T(8,128)(2,1)S(1)} %get-tuple-element.73, bf16[256,768]{1,0:T(8,128)(2,1)S(1)} %copy-done, f32[768]{0:T(1024)S(1)} %copy-done.24, f32[768]{0:T(1024)S(1)} %copy-done.21, f32[256]{0:T(256)S(1)} %copy-done.35, f32[256]{0:T(256)S(1)} %copy-done.29), kind=kOutput, calls=%fused_computation.2 | convolution fusion | flops 1211498496 | bytes 6692864 | tf_op jit(solution)/shard_map/dot_general | solution.py:492
  192.6 90.3 %shard_map.264 = (f32[96,768]{1,0:T(8,128)}, f32[96,768]{1,0:T(8,128)}, f32[96,768]{1,0:T(8,128)}, f32[72,128]{1,0:T(8,128)}) custom-call(bf16[768,3072]{1,0:T(8,128)(2,1)} %convolution_convert_fusion.2.grads_att, bf16[768,3072]{1,0:T(8,128)(2,1)} %convolution_convert_fusion.1.grads_in, bf16[768,3072]{1,0:T(8,128)(2,1)} %convolution_convert_fusion.grads_out, ...), custom_call_target="tpu_custom_call" | custom-call | tf_op jit(solution)/shard_map/pallas_call | solution.py:399
  282.9 1.4 dynamic_slice.7
  284.3 1.4 dynamic_slice.6
  285.6 1.4 slice_bitcast_fusion.6
  287.0 1.0 slice_bitcast_fusion.5
  288.0 1.7 slice.164
  291.0 1.7 copy.68
  292.7 1.7 copy.69
  (126 shorter events, 13.5 us)
Async XLA Ops:
  5.2 8.9 %copy-start.26 = (f32[256]{0:T(256)}, f32[256]{0:T(256)S(1)}, u32[]{:S(2)}) copy-start(f32[256]{0:T(256)S(1)} %broadcast_multiply_fusion.5) | copy-start | bytes 3076
  6.4 7.7 %copy-start.32 = (f32[256]{0:T(256)}, f32[256]{0:T(256)S(1)}, u32[]{:S(2)}) copy-start(f32[256]{0:T(256)S(1)} %add_rsqrt_fusion) | copy-start | bytes 3076
  14.1 84.3 %copy-start.13 = (bf16[256,768]{1,0:T(8,128)(2,1)}, bf16[256,768]{1,0:T(8,128)(2,1)S(1)}, u32[]{:S(2)}) copy-start(bf16[256,768]{1,0:T(8,128)(2,1)S(1)} %fusion.76) | copy-start | bytes 1179652
  17.9 79.9 %copy-start.1 = (bf16[256,768]{1,0:T(8,128)(2,1)}, bf16[256,768]{1,0:T(8,128)(2,1)S(1)}, u32[]{:S(2)}) copy-start(bf16[256,768]{1,0:T(8,128)(2,1)S(1)} %get-tuple-element.71) | copy-start | bytes 1179652
  93.4 1.3 copy-start.18
  98.4 12.4 %copy-start.10 = (bf16[256,4,192]{0,2,1:T(8,128)(2,1)}, bf16[256,4,192]{0,2,1:T(8,128)(2,1)S(1)}, u32[]{:S(2)}) copy-start(bf16[256,4,192]{0,2,1:T(8,128)(2,1)S(1)} %convert_element_type.150) | copy-start | bytes 1179652
  98.4 3.9 %copy-start.22 = (f32[3,12,64]{2,1,0:T(8,128)S(1)}, f32[3,12,64]{2,1,0:T(8,128)}, u32[]{:S(2)}) copy-start(f32[3,12,64]{2,1,0:T(8,128)} %add.189) | copy-start | bytes 27652
  102.7 8.1 %copy-start.7 = (bf16[256,3,12,64]{0,3,2,1:T(8,128)(2,1)}, bf16[256,3,12,64]{0,3,2,1:T(8,128)(2,1)S(1)}, u32[]{:S(2)}) copy-start(bf16[256,3,12,64]{0,3,2,1:T(8,128)(2,1)S(1)} %add_convert_fusion) | copy-start | bytes 3538948
  102.7 1.8 copy-start.17
  102.7 2.6 copy-start
  102.7 2.6 copy-start.20
  102.8 2.5 copy-start.23
  102.8 2.5 copy-start.27
  102.8 2.5 copy-start.33
  115.6 1.9 copy-start.16
  117.5 3.8 %copy-start.9 = (f32[12,256,256]{1,2,0:T(8,128)}, f32[12,256,256]{1,2,0:T(8,128)S(1)}, u32[]{:S(2)}) copy-start(f32[12,256,256]{1,2,0:T(8,128)S(1)} %get-tuple-element.102) | copy-start | bytes 9437188
  118.1 3.2 %copy-start.11 = (bf16[256,4,192]{0,2,1:T(8,128)(2,1)S(1)}, bf16[256,4,192]{0,2,1:T(8,128)(2,1)}, u32[]{:S(2)}) copy-start(bf16[256,4,192]{0,2,1:T(8,128)(2,1)} %copy-done.10) | copy-start | bytes 1179652
  118.2 3.1 %copy-start.38 = (f32[12,256]{1,0:T(8,128)}, f32[12,256]{1,0:T(8,128)S(1)}, u32[]{:S(2)}) copy-start(f32[12,256]{1,0:T(8,128)S(1)} %log_add_fusion) | copy-start | bytes 36868
  138.3 4.5 %copy-start.12 = (bf16[256,1,12,64]{0,3,2,1:T(8,128)(2,1)S(1)}, bf16[256,1,12,64]{0,3,2,1:T(8,128)(2,1)}, u32[]{:S(2)}) copy-start(bf16[256,1,12,64]{0,3,2,1:T(8,128)(2,1)} %fusion.63) | copy-start | bytes 1179652
  142.8 6.2 %copy-start.40 = (f32[4,1,768]{2,0,1:T(4,128)S(1)}, f32[4,1,768]{2,0,1:T(4,128)}, u32[]{:S(2)}) copy-start(f32[4,1,768]{2,0,1:T(4,128)} %copy.56) | copy-start | bytes 36868
  142.8 6.2 %copy-start.41 = (f32[768]{0:T(1024)S(1)}, f32[768]{0:T(1024)}, u32[]{:S(2)}) copy-start(f32[768]{0:T(1024)} %param.31) | copy-start | bytes 9220
  149.0 6.0 %copy-start.15 = (bf16[12,64,256]{2,1,0:T(8,128)(2,1)S(1)}, bf16[12,64,256]{2,1,0:T(8,128)(2,1)}, u32[]{:S(2)}) copy-start(bf16[12,64,256]{2,1,0:T(8,128)(2,1)} %convolution_convert_fusion.4) | copy-start | bytes 1179652
  149.0 6.1 %copy-start.5 = (bf16[256,3,12,64]{0,3,2,1:T(8,128)(2,1)S(1)}, bf16[256,3,12,64]{0,3,2,1:T(8,128)(2,1)}, u32[]{:S(2)}) copy-start(bf16[256,3,12,64]{0,3,2,1:T(8,128)(2,1)} %get-tuple-element.69) | copy-start | bytes 3538948
  155.0 1.0 copy-start.2
  155.0 1.1 copy-start.14
  156.2 4.5 %copy-start.8 = (f32[256,4,768]{2,0,1:T(8,128)S(1)}, f32[256,4,768]{2,0,1:T(8,128)}, u32[]{:S(2)}) copy-start(f32[256,4,768]{2,0,1:T(8,128)} %fusion.7) | copy-start | bytes 9437188
  167.5 4.4 %copy-start.6 = (bf16[256,3,12,64]{0,3,2,1:T(8,128)(2,1)S(1)}, bf16[256,3,12,64]{0,3,2,1:T(8,128)(2,1)}, u32[]{:S(2)}) copy-start(bf16[256,3,12,64]{0,3,2,1:T(8,128)(2,1)} %get-tuple-element.69) | copy-start | bytes 3538948
  167.5 4.4 %copy-start.21 = (f32[768]{0:T(1024)S(1)}, f32[768]{0:T(1024)}, u32[]{:S(2)}) copy-start(f32[768]{0:T(1024)} %param.22) | copy-start | bytes 9220
  167.5 4.4 %copy-start.28 = (f32[256]{0:T(256)S(1)}, f32[256]{0:T(256)}, u32[]{:S(2)}) copy-start(f32[256]{0:T(256)} %copy-done.26) | copy-start | bytes 3076
  167.6 4.4 %copy-start.34 = (f32[256]{0:T(256)S(1)}, f32[256]{0:T(256)}, u32[]{:S(2)}) copy-start(f32[256]{0:T(256)} %copy-done.32) | copy-start | bytes 3076
  167.6 4.4 %copy-start.36 = (f32[768]{0:T(1024)S(1)}, f32[768]{0:T(1024)}, u32[]{:S(2)}) copy-start(f32[768]{0:T(1024)} %param.20) | copy-start | bytes 9220
  171.9 3.9 %copy-start.30 = (f32[9216]{0:T(1024)S(1)}, f32[9216]{0:T(1024)}, u32[]{:S(2)}) copy-start(f32[9216]{0:T(1024)} %custom-call) | copy-start | bytes 110596
  172.0 3.9 %copy-start.37 = (f32[768]{0:T(1024)S(1)}, f32[768]{0:T(1024)}, u32[]{:S(2)}) copy-start(f32[768]{0:T(1024)} %get-tuple-element.70) | copy-start | bytes 9220
  172.0 3.9 %copy-start.25 = (f32[2304]{0:T(1024)S(1)}, f32[2304]{0:T(1024)}, u32[]{:S(2)}) copy-start(f32[2304]{0:T(1024)} %reduce_sum.153) | copy-start | bytes 27652
  172.0 4.6 %copy-start.3 = (bf16[256,768]{1,0:T(8,128)(2,1)S(1)}, bf16[256,768]{1,0:T(8,128)(2,1)}, u32[]{:S(2)}) copy-start(bf16[256,768]{1,0:T(8,128)(2,1)} %copy-done.1) | copy-start | bytes 1179652
  175.9 0.6 copy-start.31
  177.9 3.5 %copy-start.19 = (f32[4,1,768]{2,1,0:T(1,128)S(1)}, f32[4,1,768]{2,1,0:T(1,128)}, u32[]{:S(2)}) copy-start(f32[4,1,768]{2,1,0:T(1,128)} %copy-done.18) | copy-start | bytes 36868
  181.4 3.8 %copy-start.4 = (bf16[256,768]{1,0:T(8,128)(2,1)S(1)}, bf16[256,768]{1,0:T(8,128)(2,1)}, u32[]{:S(2)}) copy-start(bf16[256,768]{1,0:T(8,128)(2,1)} %copy-done.1) | copy-start | bytes 1179652
  185.2 3.7 %copy-start.24 = (f32[768]{0:T(1024)S(1)}, f32[768]{0:T(1024)}, u32[]{:S(2)}) copy-start(f32[768]{0:T(1024)} %param.23) | copy-start | bytes 9220
  185.2 3.6 %copy-start.29 = (f32[256]{0:T(256)S(1)}, f32[256]{0:T(256)}, u32[]{:S(2)}) copy-start(f32[256]{0:T(256)} %copy-done.26) | copy-start | bytes 3076
  185.2 3.6 %copy-start.35 = (f32[256]{0:T(256)S(1)}, f32[256]{0:T(256)}, u32[]{:S(2)}) copy-start(f32[256]{0:T(256)} %copy-done.32) | copy-start | bytes 3076
  287.0 7.4 %copy-start.39 = (f32[768]{0:T(1024)}, f32[768]{0:T(1024)S(1)}, u32[]{:S(2)}) copy-start(f32[768]{0:T(1024)S(1)} %get-tuple-element.158) | copy-start | bytes 9220
